TPU v7x, 256 devices: a whole 4x4x8 slice. The times are simulated.
256 devices in a mesh: probe: 4 (over y_lo, core), tile: 32 (over z, x), level: 2 (over y_hi).
Axes of the slice: x: 4, y: 4 (y_hi: 2, y_lo: 2; y = y_hi * 2 + y_lo), z: 8, core: 2. Of those that a mesh axis runs over, the one named last changes fastest.
Arguments:
- probe_bits: int32 [4, 64, 256, 256], P('probe', 'level', 'tile'), may hold values from 0 to 1
- kappa_sq: float32 [64, 256, 256], P('level', 'tile'), may hold values from 0.25 to 4
- observed: float32 [64, 256, 256], P('level', 'tile'), may hold values from -0.6 to 0.6
Outputs:
- gradient: float32 [64, 256, 256], P('level', 'tile', 'probe')
Inputs may be any that keep to these rules, and one draw needn't show every extreme that they name: `probe_bits`: a probe's sign is 2 times its bit minus 1.
All inputs are finite; a program needn't handle non-finite values.
Results may differ from a plain program's by a relative error of at most 0.0003.
Values sent between devices are 32-bit elements; how exact they have to be, the bound alone decides.
A program may use at most 64 MiB of HBM per device.

v0:
```python
import jax
import jax.numpy as jnp
from jax import lax
from jax.sharding import PartitionSpec as P

ITERS = 4


VERTICAL = 2.0


def with_halo(cells, sides, width):
    for axis, dim in sides:
        count = lax.axis_size(axis)
        ends = count - 1
        head = lax.slice_in_dim(cells, 0, width, axis=dim)
        tail = lax.slice_in_dim(cells, cells.shape[dim] - width, cells.shape[dim], axis=dim)
        cells = jnp.concatenate(
            [
                lax.ppermute(tail, axis, [(i, (i + 1) % count) for i in range(ends)]),
                cells,
                lax.ppermute(head, axis, [((i + 1) % count, i) for i in range(ends)]),
            ],
            axis=dim,
        )
    return cells


def shift_levels(values, stride, level_dim, fill_value):
    level_count = values.shape[level_dim]
    widths = [(0, 0)] * values.ndim
    if stride > 0:
        widths[level_dim] = (stride, 0)
        padded = jnp.pad(values, widths, constant_values=fill_value)
        return lax.slice_in_dim(padded, 0, level_count, axis=level_dim)
    widths[level_dim] = (0, -stride)
    padded = jnp.pad(values, widths, constant_values=fill_value)
    return lax.slice_in_dim(padded, -stride, level_count - stride, axis=level_dim)


def reduction_tables(kappa_sq):
    level_count = kappa_sq.shape[0]
    level_ids = lax.broadcasted_iota(jnp.int32, kappa_sq.shape, 0)
    diagonal = kappa_sq + (4.0 + 2.0 * VERTICAL)
    lower = jnp.where(level_ids > 0, -VERTICAL, 0.0).astype(jnp.float32)
    upper = jnp.where(level_ids < level_count - 1, -VERTICAL, 0.0).astype(jnp.float32)
    tables = []
    stride = 1
    while stride < level_count:
        lower_ratio = -lower / shift_levels(diagonal, stride, 0, 1.0)
        upper_ratio = -upper / shift_levels(diagonal, -stride, 0, 1.0)
        new_diagonal = (
            diagonal
            + lower_ratio * shift_levels(upper, stride, 0, 0.0)
            + upper_ratio * shift_levels(lower, -stride, 0, 0.0)
        )
        new_lower = lower_ratio * shift_levels(lower, stride, 0, 0.0)
        upper = upper_ratio * shift_levels(upper, -stride, 0, 0.0)
        lower = new_lower
        diagonal = new_diagonal
        tables.append((lower_ratio, upper_ratio, stride))
        stride = stride * 2
    return (tables, 1.0 / diagonal)


def vertical_solve(values, tables, inverse_diagonal):
    for lower_ratio, upper_ratio, stride in tables:
        values = (
            values
            + lower_ratio * shift_levels(values, stride, 1, 0.0)
            + upper_ratio * shift_levels(values, -stride, 1, 0.0)
        )
    return values * inverse_diagonal


def stencil(padded, values, kappa_sq):
    beside_x = padded[:, 1:-1, 2:, 1:-1] + padded[:, 1:-1, :-2, 1:-1]
    beside_y = padded[:, 1:-1, 1:-1, 2:] + padded[:, 1:-1, 1:-1, :-2]
    beside_z = padded[:, 2:, 1:-1, 1:-1] + padded[:, :-2, 1:-1, 1:-1]
    return (kappa_sq + (4.0 + 2.0 * VERTICAL)) * values - beside_x - beside_y - VERTICAL * beside_z


def slab_apply(values, kappa_sq):
    extended = with_halo(values, (("tile", 2), ("level", 1)), 1)
    padded = jnp.pad(extended, ((0, 0), (0, 0), (0, 0), (1, 1)))
    return stencil(padded, values, kappa_sq)


def local_dots(first, second):
    return jnp.sum(first * second, axis=(1, 2, 3))


def precond_total(residual, precond):
    return lax.psum(local_dots(residual, precond), ("tile", "level"))


def conjugate_solve(right_side, apply_q, apply_m):
    shaped = (right_side.shape[0], 1, 1, 1)
    solution = jnp.zeros_like(right_side)
    residual = right_side
    precond = apply_m(residual)
    rho_now = precond_total(residual, precond)
    direction = precond
    for iteration in range(ITERS):
        image_field = apply_q(direction)
        curv_total = lax.psum(local_dots(direction, image_field), ("tile", "level"))
        step_size = (rho_now / curv_total).reshape(shaped)
        solution = solution + step_size * direction
        if iteration + 1 < ITERS:
            residual = residual - step_size * image_field
            precond = apply_m(residual)
            rho_next = precond_total(residual, precond)
            direction = precond + (rho_next / rho_now).reshape(shaped) * direction
            rho_now = rho_next
    return solution


def body(probe_bits, kappa_sq, observed):
    sign_field = (2 * probe_bits - 1).astype(jnp.float32)
    stacked = jnp.concatenate([sign_field, observed[None]], axis=0)
    extended = with_halo(stacked, (("tile", 2), ("level", 1)), 1)
    padded = jnp.pad(extended, ((0, 0), (0, 0), (0, 0), (1, 1)))
    k_stacked = stencil(padded, stacked, kappa_sq)
    k_signs = k_stacked[:-1]
    data_term = 2.0 * observed * k_stacked[-1]
    kappa_cols = lax.all_to_all(kappa_sq[None], "level", split_axis=3, concat_axis=1, tiled=True)[0]
    tables, inverse_diagonal = reduction_tables(kappa_cols)

    def solve_columns(columns):
        solved = vertical_solve(
            vertical_solve(columns, tables, inverse_diagonal), tables, inverse_diagonal
        )
        return lax.all_to_all(solved, "level", split_axis=1, concat_axis=3, tiled=True)

    def apply_m(values):
        return solve_columns(
            lax.all_to_all(values, "level", split_axis=3, concat_axis=1, tiled=True)
        )

    def apply_q(values):
        return slab_apply(slab_apply(values, kappa_sq), kappa_sq)

    solution = conjugate_solve(sign_field, apply_q, apply_m)
    probe_partial = jnp.sum(
        solution * k_signs + slab_apply(solution, kappa_sq) * sign_field, axis=0
    )
    summed = lax.psum_scatter(probe_partial, "probe", scatter_dimension=2, tiled=True)
    y_width = summed.shape[2]
    offset = lax.axis_index("probe") * y_width
    kappa_part = lax.dynamic_slice_in_dim(kappa_sq, offset, y_width, 2)
    data_part = lax.dynamic_slice_in_dim(data_term, offset, y_width, 2)
    probe_count = probe_bits.shape[0] * lax.axis_size("probe")
    return kappa_part * (summed / probe_count - data_part)


def solution(mesh):
    in_specs = (
        P("probe", "level", "tile", None),
        P("level", "tile", None),
        P("level", "tile", None),
    )
    out_specs = P("level", "tile", "probe")
    return jax.shard_map(body, mesh=mesh, in_specs=in_specs, out_specs=out_specs, check_vma=False)
```

profile of v0, /device:TPU:1, one launch (start us, length us, event | category | flops | bytes accessed | tf_op | source)
XLA Modules:
  0.0 1670.7 jit_solution(17637381411247329690)
XLA Ops:
  9.1 5.0 all-to-all-start.1
  15.8 3.9 all-to-all-done.1
  19.7 3.4 all-to-all-start
  26.1 2.6 all-to-all-done
  33.5 8.0 all_to_all.165
  43.0 4.0 collective-permute-start.1
  48.0 1.9 collective-permute-start.2
  51.2 4.7 collective-permute-done.3
  58.1 4.3 collective-permute-start.5
  66.3 4.7 collective-permute-done.7
  73.2 158.1 %all-reduce.140 = (f32[1]{0:T(128)}, f32[1]{0:T(128)}) all-reduce(f32[1]{0:T(128)} %bitcast.26, f32[1]{0:T(128)} %bitcast.30), channel_id=1, replica_groups=mesh['probe'=4,'tile'=32,'level'=2] {'tile','level'}, use_global_device_ids=true, to_apply=%region_1.2 | all-reduce | flops 2 | bytes 16 | tf_op jit(solution)/shard_map/psum | solution.py:94
  232.6 1.8 multiply_subtract_fusion.2
  234.4 2.3 copy.53
  236.7 2.4 reshape.183
  239.0 9.9 all_to_all.166
  249.0 3.1 reduce.10
  252.0 2.4 reshape.184
  254.4 2.2 copy.54
  259.4 8.0 all_to_all.167
  268.1 149.1 %psum.58 = f32[1]{0:T(128)} all-reduce(f32[1]{0:T(128)} %bitcast.39), channel_id=1, replica_groups=mesh['probe'=4,'tile'=32,'level'=2] {'tile','level'}, use_global_device_ids=true, to_apply=%region_5.6 | all-reduce | flops 1 | bytes 8 | tf_op jit(solution)/shard_map/psum | solution.py:94
  420.8 4.0 collective-permute-start.9
  425.9 5.0 collective-permute-start.10
  432.2 5.0 collective-permute-done.11
  440.1 4.0 collective-permute-start.13
  448.0 4.7 collective-permute-done.15
  454.8 149.1 %psum.59 = f32[1]{0:T(128)} all-reduce(f32[1]{0:T(128)} %bitcast.43), channel_id=1, replica_groups=mesh['probe'=4,'tile'=32,'level'=2] {'tile','level'}, use_global_device_ids=true, to_apply=%region_7.8 | all-reduce | flops 1 | bytes 8 | tf_op jit(solution)/shard_map/psum | solution.py:106
  605.2 1.8 multiply_subtract_fusion.1
  607.0 2.3 copy.59
  609.3 2.4 reshape.185
  611.7 10.3 all_to_all.168
  622.0 3.1 reduce.11
  625.1 2.4 reshape.186
  627.5 2.2 copy.60
  632.5 7.9 all_to_all.169
  641.7 149.8 %psum.60 = f32[1]{0:T(128)} all-reduce(f32[1]{0:T(128)} %bitcast.52), channel_id=1, replica_groups=mesh['probe'=4,'tile'=32,'level'=2] {'tile','level'}, use_global_device_ids=true, to_apply=%region_9.10 | all-reduce | flops 1 | bytes 8 | tf_op jit(solution)/shard_map/psum | solution.py:94
  795.2 4.0 collective-permute-start.17
  800.2 4.4 collective-permute-start.18
  805.9 4.7 collective-permute-done.19
  812.8 4.3 collective-permute-start.21
  821.1 5.0 collective-permute-done.23
  828.2 149.4 %psum.61 = f32[1]{0:T(128)} all-reduce(f32[1]{0:T(128)} %bitcast.56), channel_id=1, replica_groups=mesh['probe'=4,'tile'=32,'level'=2] {'tile','level'}, use_global_device_ids=true, to_apply=%region_11.12 | all-reduce | flops 1 | bytes 8 | tf_op jit(solution)/shard_map/psum | solution.py:106
  978.9 1.8 multiply_subtract_fusion
  980.6 2.3 copy.65
  982.9 2.4 reshape.187
  985.3 10.2 all_to_all.170
  995.5 3.1 reduce.12
  998.6 2.4 reshape.188
  1001.0 2.2 copy.66
  1006.0 8.1 all_to_all.171
  1014.8 150.4 %psum.62 = f32[1]{0:T(128)} all-reduce(f32[1]{0:T(128)} %bitcast.65), channel_id=1, replica_groups=mesh['probe'=4,'tile'=32,'level'=2] {'tile','level'}, use_global_device_ids=true, to_apply=%region_13.14 | all-reduce | flops 1 | bytes 8 | tf_op jit(solution)/shard_map/psum | solution.py:94
  1167.8 4.0 collective-permute-start.25
  1172.9 4.1 collective-permute-start.26
  1179.7 4.3 collective-permute-start.33
  1186.2 4.0 collective-permute-start.29
  1191.2 5.6 collective-permute-start.30
  1198.2 5.5 collective-permute-start.34
  1206.5 152.8 %psum.63 = f32[1]{0:T(128)} all-reduce(f32[1]{0:T(128)} %bitcast.69), channel_id=1, replica_groups=mesh['probe'=4,'tile'=32,'level'=2] {'tile','level'}, use_global_device_ids=true, to_apply=%region_15.16 | all-reduce | flops 1 | bytes 8 | tf_op jit(solution)/shard_map/psum | solution.py:106
  1362.0 4.0 collective-permute-start.37
  1367.1 1.9 collective-permute-start.38
  1369.0 1.7 collective-permute-start.39
  1371.2 3.9 collective-permute-done.39
  1376.1 4.4 copy.71
  1380.5 4.7 reshape.177
  1385.2 275.9 %reduce-scatter.4.cloned.1.call-done = f32[64,256]{1,0:T(8,128)} async-done(((f32[256,256]{1,0:T(8,128)}), f32[64,256]{1,0:T(8,128)}) %reduce-scatter.4.cloned.1.call-update) | async-done | bytes 65552
  (237 shorter events, 79.9 us)
Async XLA Ops:
  7.9 6.2 copy-start.15
  9.1 10.5 all-to-all-start.1
  14.2 11.0 copy-start.9
  19.7 9.0 all-to-all-start
  23.1 1637.9 %reduce-scatter.4.cloned.1.call-start = ((), (), s32[]{:S(2)}) async-start(), calls=%async_computation.10 | async-start | bytes 327680
  33.5 22.9 %copy-start = (f32[32,8,256]{2,1,0:T(8,128)S(1)}, f32[32,8,256]{2,1,0:T(8,128)}, u32[]{:S(2)}) copy-start(f32[32,8,256]{2,1,0:T(8,128)} %param.4) | copy-start | bytes 786436
  41.7 5.3 collective-permute-start
  43.0 5.0 collective-permute-start.1
  48.0 3.2 collective-permute-start.2
  49.9 6.0 collective-permute-start.3
  56.4 15.1 copy-start.16
  56.8 5.6 collective-permute-start.4
  58.1 5.3 collective-permute-start.5
  63.4 3.0 collective-permute-start.6
  65.0 6.0 collective-permute-start.7
  257.9 1.0 copy-start.2
  259.3 8.1 copy-start.18
  417.2 20.5 %copy-start.21 = (f32[1,64,8,128]{3,2,0,1:T(8,128)S(1)}, f32[1,64,8,128]{3,2,0,1:T(8,128)}, u32[]{:S(2)}) copy-start(f32[1,64,8,128]{3,2,0,1:T(8,128)} %copy-done.20) | copy-start | bytes 786436
  419.5 33.8 %copy-start.5 = (f32[1,32,8,256]{3,2,1,0:T(8,128)}, f32[1,32,8,256]{3,2,1,0:T(8,128)S(1)}, u32[]{:S(2)}) copy-start(f32[1,32,8,256]{3,2,1,0:T(8,128)S(1)} %bitcast_add_fusion.5) | copy-start | bytes 786436
  419.5 5.3 collective-permute-start.8
  420.8 5.0 collective-permute-start.9
  425.9 6.3 collective-permute-start.10
  430.9 6.3 collective-permute-start.11
  438.8 5.3 collective-permute-start.12
  440.1 5.0 collective-permute-start.13
  445.1 2.9 collective-permute-start.14
  446.7 6.0 collective-permute-start.15
  632.3 8.7 copy-start.19
  791.5 19.6 %copy-start.12 = (f32[1,64,8,128]{3,2,0,1:T(8,128)S(1)}, f32[1,64,8,128]{3,2,0,1:T(8,128)}, u32[]{:S(2)}) copy-start(f32[1,64,8,128]{3,2,0,1:T(8,128)} %copy-done.11) | copy-start | bytes 786436
  791.5 19.6 %copy-start.22 = (f32[32,8,256]{2,1,0:T(8,128)S(1)}, f32[32,8,256]{2,1,0:T(8,128)}, u32[]{:S(2)}) copy-start(f32[32,8,256]{2,1,0:T(8,128)} %get-tuple-element.14) | copy-start | bytes 786436
  793.9 32.7 %copy-start.7 = (f32[1,32,8,256]{3,2,1,0:T(8,128)}, f32[1,32,8,256]{3,2,1,0:T(8,128)S(1)}, u32[]{:S(2)}) copy-start(f32[1,32,8,256]{3,2,1,0:T(8,128)S(1)} %bitcast_add_fusion.3) | copy-start | bytes 786436
  793.9 5.3 collective-permute-start.16
  795.2 5.0 collective-permute-start.17
  800.2 5.7 collective-permute-start.18
  804.6 6.0 collective-permute-start.19
  811.5 5.6 collective-permute-start.20
  812.8 5.3 collective-permute-start.21
  818.1 3.0 collective-permute-start.22
  819.7 6.3 collective-permute-start.23
  1004.5 1.0 copy-start.4
  1005.9 8.3 copy-start.24
  1005.9 160.6 %copy-start.8 = (f32[1,32,8,256]{3,2,1,0:T(8,128)S(1)}, f32[1,32,8,256]{3,2,1,0:T(8,128)}, u32[]{:S(2)}) copy-start(f32[1,32,8,256]{3,2,1,0:T(8,128)} %copy-done.7) | copy-start | bytes 786436
  1005.9 172.4 %copy-start.10 = (f32[1,32,8,256]{3,2,1,0:T(8,128)S(1)}, f32[1,32,8,256]{3,2,1,0:T(8,128)}, u32[]{:S(2)}) copy-start(f32[1,32,8,256]{3,2,1,0:T(8,128)} %copy-done.9) | copy-start | bytes 786436
  1005.9 172.4 %copy-start.14 = (f32[32,8,256]{2,1,0:T(8,128)S(1)}, f32[32,8,256]{2,1,0:T(8,128)}, u32[]{:S(2)}) copy-start(f32[32,8,256]{2,1,0:T(8,128)} %param.5) | copy-start | bytes 786436
  1014.8 169.8 %copy-start.13 = (f32[1,64,8,128]{3,2,0,1:T(8,128)S(1)}, f32[1,64,8,128]{3,2,0,1:T(8,128)}, u32[]{:S(2)}) copy-start(f32[1,64,8,128]{3,2,0,1:T(8,128)} %copy-done.11) | copy-start | bytes 786436
  1014.8 169.8 %copy-start.23 = (f32[32,8,256]{2,1,0:T(8,128)S(1)}, f32[32,8,256]{2,1,0:T(8,128)}, u32[]{:S(2)}) copy-start(f32[32,8,256]{2,1,0:T(8,128)} %get-tuple-element.14) | copy-start | bytes 786436
  1166.5 5.3 collective-permute-start.24
  1167.8 5.0 collective-permute-start.25
  1172.9 11.1 collective-permute-start.26
  1177.0 7.0 collective-permute-start.27
  1178.4 19.8 %collective-permute-start.32 = (f32[2,32,1,256]{3,2,1,0:T(1,128)S(1)}, f32[2,32,1,256]{3,2,1,0:T(1,128)S(1)}, u32[]{:S(2)}, u32[]{:S(2)}) collective-permute-start(f32[2,32,1,256]{3,2,1,0:T(1,128)S(1)} %get-tuple-element.47), channel_id=1, source_target_pairs={{2,0},{4,2},{6,4},{8,6},{10,8},{12,10},{14,12},{16,14},{18,16},{20... | collective-permute-start | bytes 196616 | tf_op jit(solution)/shard_map/ppermute | solution.py:22
  1179.7 18.5 %collective-permute-start.33 = (f32[2,32,1,256]{3,2,1,0:T(1,128)S(1)}, f32[2,32,1,256]{3,2,1,0:T(1,128)S(1)}, u32[]{:S(2)}, u32[]{:S(2)}) collective-permute-start(f32[2,32,1,256]{3,2,1,0:T(1,128)S(1)} %get-tuple-element.46), channel_id=1, source_target_pairs={{0,2},{2,4},{4,6},{6,8},{8,10},{10,12},{12,14},{14,16},{16,18},{18... | collective-permute-start | bytes 196616 | tf_op jit(solution)/shard_map/ppermute | solution.py:20
  1184.9 5.3 collective-permute-start.28
  1186.2 5.0 collective-permute-start.29
  1191.2 169.4 %copy-start.6 = (f32[1,32,8,256]{3,2,1,0:T(8,128)S(1)}, f32[1,32,8,256]{3,2,1,0:T(8,128)}, u32[]{:S(2)}) copy-start(f32[1,32,8,256]{3,2,1,0:T(8,128)} %copy-done.5) | copy-start | bytes 786436
  1191.2 13.8 collective-permute-start.30
  1196.9 8.2 collective-permute-start.31
  1198.2 167.8 %collective-permute-start.34 = (f32[2,1,10,256]{3,2,1,0:T(8,128)S(1)}, f32[2,1,10,256]{3,2,1,0:T(8,128)S(1)}, u32[]{:S(2)}, u32[]{:S(2)}) collective-permute-start(f32[2,1,10,256]{3,2,1,0:T(8,128)S(1)} %get-tuple-element.39), channel_id=1, source_target_pairs={{0,1},{2,3},{4,5},{6,7},{8,9},{10,11},{12,13},{14,15},{16,17},{18,... | collective-permute-start | bytes 61448 | tf_op jit(solution)/shard_map/ppermute | solution.py:20
  1203.7 162.3 %collective-permute-start.35 = (f32[2,1,10,256]{3,2,1,0:T(8,128)S(1)}, f32[2,1,10,256]{3,2,1,0:T(8,128)S(1)}, u32[]{:S(2)}, u32[]{:S(2)}) collective-permute-start(f32[2,1,10,256]{3,2,1,0:T(8,128)S(1)} %get-tuple-element.38), channel_id=1, source_target_pairs={{1,0},{3,2},{5,4},{7,6},{9,8},{11,10},{13,12},{15,14},{17,16},{19,... | collective-permute-start | bytes 61448 | tf_op jit(solution)/shard_map/ppermute | solution.py:22
  1360.7 6.3 collective-permute-start.36
  1362.0 5.0 collective-permute-start.37
  1367.1 4.1 collective-permute-start.38
  1369.0 6.7 copy-start.17
  1369.0 6.1 collective-permute-start.39
  (4 other events, 3.1 us)
Sparse Core Ops, SparseCore 0:
  1385.3 275.7 reduce-scatter.3
where the time goes:
time: 1670 us
  blocking collectives  1120 us (67%)
  waiting for transfers between devices  323 us (19%)
  starting transfers between devices  109 us (7%)
  local copies, waits for them, and re-layouts  52.3 us (3%)
  other arithmetic  41.6 us (2%)
  between operations  23.8 us (1%)
    psum x4, blocking collectives, precond_total(): return lax.psum(local_dots(residual, precond), ('tile', 'level'))  607 us
    psum x3, blocking collectives, conjugate_solve(): curv_total = lax.psum(local_dots(direction, image_field), ('tile', 'level'))  451 us
    unnamed x2, waiting for transfers between devices  276 us
    ppermute x20, starting transfers between devices, with_halo(): lax.ppermute(tail, axis, [(i, (i + 1) % count) for i in range(ends)])  74.2 us
  transfers between devices with their start and end apart: 43, of which 18 were waited for; matrix products, arithmetic and copies ran while one was open for 1% of the time, Pallas kernels for 0%

commit v1 on v0

v1 whole, which is shorter than its diff:
```python
import functools

import jax
import jax.numpy as jnp
from jax import lax
from jax.experimental import pallas as pl
from jax.experimental.pallas import tpu as pltpu
from jax.sharding import PartitionSpec as P

MESH = pl.DeviceIdType.MESH
STEPS = 4
F32 = jnp.float32
X_CHIPS = 4

PAIRS = [(i, j) for j in range(STEPS) for i in range(j + 1)]
ROW = {pair: n for n, pair in enumerate(PAIRS)}
N_ROWS = 16


def kernel(
    dims,
    bits_hbm, kap_hbm, obs_hbm, out_ref,
    bits_v, kap_v, obs_v,
    s_m, s_h, d_m, d_h, o_m, o_h,
    m_m, m_h, hg_m, hg_h,
    v_m, v_h, u_m, u_h, r_m, r_h, f_m, f_h, ks, data,
    halo_out, halo_in, xs_out, xs_in,
    setup_m_out, setup_m_in, setup_h_out, setup_h_in,
    pl_out, pl_in,
    gram, red_a, red_b, rs_out, rs_in,
    in_sem, send_sem, recv_sem, sa_sem, ra_sem, sb_sem, rb_sem, sp_sem, rp_sem,
):
    probes, tiles, levels, x_chips, L, Y = dims
    z_chips = tiles // x_chips
    probe = lax.axis_index("probe")
    tile = lax.axis_index("tile")
    half = lax.axis_index("level")
    zc = tile // x_chips
    xc = tile % x_chips
    nxt = lax.rem(tile + 1, tiles)
    prv = lax.rem(tile + tiles - 1, tiles)
    other = 1 - half
    grp = half * x_chips + xc
    n_a = levels * x_chips

    loads = [
        pltpu.make_async_copy(kap_hbm, kap_v, in_sem.at[0]),
        pltpu.make_async_copy(bits_hbm.at[0], bits_v, in_sem.at[1]),
        pltpu.make_async_copy(obs_hbm, obs_v, in_sem.at[2]),
    ]
    for copy in loads:
        copy.start()

    a_peers = []
    for k in range(1, n_a):
        g = lax.rem(grp + k, n_a)
        a_peers.append((g, {"tile": zc * x_chips + g % x_chips, "level": g // x_chips}))
    b_peers = []
    for k in range(1, z_chips):
        g = lax.rem(zc + k, z_chips)
        b_peers.append((g, {"tile": g * x_chips + xc}))
    p_peers = []
    for k in range(1, probes):
        g = lax.rem(probe + k, probes)
        p_peers.append((g, {"probe": g}))

    barrier = pltpu.get_barrier_semaphore()
    greet = [{"tile": nxt}, {"tile": prv}, {"level": other},
             {"tile": nxt, "level": other}, {"tile": prv, "level": other}]
    greet += [d for _, d in a_peers] + [d for _, d in b_peers] + [d for _, d in p_peers]
    for dev in greet:
        pl.semaphore_signal(barrier, inc=1, device_id=dev, device_id_type=MESH)

    sub = lax.broadcasted_iota(jnp.int32, (8, Y), 0)
    lane = lax.broadcasted_iota(jnp.int32, (8, Y), 1)
    lane_h = lax.broadcasted_iota(jnp.int32, (8, 128), 1)
    has_next = (tile < tiles - 1).astype(F32)
    has_prev = (tile > 0).astype(F32)
    mask_h = jnp.where(sub < 2, has_next, jnp.where(sub >= 6, has_prev, 0.0))
    zero = jnp.zeros((8, Y), F32)

    def src(l):
        return half * (L - 1) + (1 - 2 * half) * l

    def send(src_ref, dst_ref, ssem, rsem, dev):
        copy = pltpu.make_async_remote_copy(
            src_ref=src_ref, dst_ref=dst_ref, send_sem=ssem, recv_sem=rsem,
            device_id=dev, device_id_type=MESH)
        copy.start()
        return copy

    started = []
    counter = [0]

    def post(src_ref, dst_ref, dev):
        n = counter[0]
        counter[0] += 1
        copy = send(src_ref, dst_ref, send_sem.at[n], recv_sem.at[n], dev)
        started.append(copy)
        return copy

    def loop(n, chunk, body, init=0):
        chunk = min(chunk, n)

        def step(b, carry):
            for k in range(chunk):
                carry = body(b * chunk + k, carry)
            return carry

        return lax.fori_loop(0, n // chunk, step, init)

    def each(n, chunk, body):
        def step(l, carry):
            body(l)
            return carry
        loop(n, chunk, step)

    def pack(read, up_ref, dn_ref):
        def body(g):
            rows = [read(4 * g + k) for k in range(4)]
            up = rows[3]
            dn = pltpu.roll(rows[3], 6, 0)
            for k in (2, 1, 0):
                up = jnp.where(sub < 2 * k + 2, pltpu.roll(rows[k], 2 * k + 2, 0), up)
                dn = jnp.where(sub < 2 * k + 2, pltpu.roll(rows[k], 2 * k, 0) if k else rows[k], dn)
            up_ref[g] = up
            dn_ref[g] = dn
        each(L // 4, 2, body)

    def unpack(a_ref, b_ref, write):
        def body(g):
            a = a_ref[g]
            b = b_ref[g]
            for k in range(4):
                ra = pltpu.roll(a, 6 - 2 * k, 0) if k < 3 else a
                rb = pltpu.roll(b, 8 - 2 * k, 0) if k else b
                write(4 * g + k, jnp.where(sub >= 4, ra, rb))
        each(L // 4, 2, body)

    def beside(a, b):
        up = jnp.where(sub == 0, pltpu.roll(b, 1, 0), pltpu.roll(a, 1, 0))
        dn = jnp.where(sub == 7, pltpu.roll(b, 7, 0), pltpu.roll(a, 7, 0))
        left = jnp.where(lane == 0, 0.0, pltpu.roll(a, 1, 1))
        right = jnp.where(lane == Y - 1, 0.0, pltpu.roll(a, Y - 1, 1))
        return (up + dn) + (left + right)

    def factor(d_ref, m_ref, hg_ref):
        m_ref[0] = zero

        def up(l, m):
            m = 2.0 / (d_ref[l] - 2.0 * m)
            m_ref[l + 1] = m
            return m
        last = loop(L, 4, up, zero)

        def down(k, h):
            l = L - 1 - k
            h = m_ref[l + 1] * h
            hg_ref[l] = h
            return h
        loop(L, 4, down, zero + 1.0)

        def again(l, g):
            g = 0.5 * hg_ref[l] + m_ref[l] * g
            hg_ref[l] = g
            return g
        return last, loop(L, 4, again, zero)

    def passes(read, m_ref, f_ref):
        def fwd(l, f):
            f = 0.5 * read(l) + m_ref[l] * f
            f_ref[l] = f
            return f
        first = loop(L, 8, fwd, zero)

        def back(k, y):
            l = L - 1 - k
            y = m_ref[l + 1] * (f_ref[l] + y)
            f_ref[l] = y
            return y
        loop(L, 8, back, zero)

        def again(l, g):
            g = 0.5 * f_ref[l] + m_ref[l] * g
            f_ref[l] = g
            return g
        return first, loop(L, 8, again, zero)

    def join(const, own, far):
        mo, ho, mp, hp, inv = const
        (fo, go), (fp, gp) = own, far
        x = mo * (fo + mp * fp) * inv
        xi = mp * (fp + mo * fo) * inv
        g = go + xi * ho
        gf = gp + x * hp
        w = mo * (g + mp * gf) * inv
        eta = mp * (gf + mo * g) * inv
        return xi, w, eta

    loads[0].wait()

    def put_d(l):
        d_m[l] = kap_v[src(l)] + 8.0
    each(L, 4, put_d)
    pack(lambda l: d_m[l], halo_out.at[0, 0], halo_out.at[1, 0])
    loads[1].wait()

    def put_s(l):
        s_m[l + 1] = (2 * bits_v[src(l)] - 1).astype(F32)
    each(L, 4, put_s)
    pack(lambda l: s_m[l + 1], halo_out.at[0, 1], halo_out.at[1, 1])
    loads[2].wait()

    def put_o(l):
        o_m[l + 1] = obs_v[src(l)]
    each(L, 4, put_o)
    pack(lambda l: o_m[l + 1], halo_out.at[0, 2], halo_out.at[1, 2])

    pl.semaphore_wait(barrier, len(greet))
    first = pl.ds(0, 2)
    halo = [
        post(halo_out.at[0, first], halo_in.at[0, first], {"tile": nxt}),
        post(halo_out.at[1, first], halo_in.at[1, first], {"tile": prv}),
    ]
    s_m[0] = zero
    o_m[0] = zero
    for j in range(STEPS):
        v_m[j, 0] = zero
        u_m[j, 0] = zero
    v_h[0] = zero

    mo_m, ho_m = factor(d_m, m_m, hg_m)
    own_m = passes(lambda l: s_m[l + 1], m_m, f_m)
    for n, plane in enumerate((mo_m, ho_m, d_m[L - 1], own_m[0], own_m[1], s_m[L], o_m[L])):
        setup_m_out[n] = plane
    far_m = post(setup_m_out, setup_m_in, {"level": other})
    late = [
        post(halo_out.at[0, 2], halo_in.at[0, 2], {"tile": nxt}),
        post(halo_out.at[1, 2], halo_in.at[1, 2], {"tile": prv}),
    ]

    for copy in halo:
        copy.wait_recv()

    def put_dh(l, x):
        d_h[l] = jnp.where(mask_h > 0.0, x, 8.0)
    unpack(halo_in.at[0, 0], halo_in.at[1, 0], put_dh)

    def put_sh(l, x):
        s_h[l] = x * mask_h
    unpack(halo_in.at[0, 1], halo_in.at[1, 1], put_sh)
    mo_h, ho_h = factor(d_h, m_h, hg_h)
    own_h = passes(lambda l: s_h[l], m_h, f_h)
    for n, plane in enumerate((mo_h, ho_h, own_h[0], own_h[1])):
        setup_h_out[n] = plane
    far_h = post(setup_h_out, setup_h_in, {"level": other})

    far_m.wait_recv()
    mp_m, hp_m, dp_m, fp_m, gp_m = (setup_m_in[n] for n in range(5))
    d_m[L] = dp_m
    s_m[L + 1] = setup_m_in[5]
    o_m[L + 1] = setup_m_in[6]
    far_h.wait_recv()
    mp_h, hp_h, fp_h, gp_h = (setup_h_in[n] for n in range(4))
    const_m = (mo_m, ho_m, mp_m, hp_m, 1.0 / (1.0 - mo_m * mp_m))
    const_h = (mo_h, ho_h, mp_h, hp_h, 1.0 / (1.0 - mo_h * mp_h))

    def finish(j, own_m, own_h, fp_m, gp_m, fp_h, gp_h):
        xi, w, eta = join(const_m, own_m, (fp_m, gp_m))
        beyond = 0.5 * (dp_m * eta - xi) - w
        v_m[j, L + 1] = eta if j == 0 else eta - v_m[j - 1, L + 1]
        v_m[j, L + 2] = beyond if j == 0 else beyond - v_m[j - 1, L + 2]

        def down_m(k, w):
            l = L - 1 - k
            w = m_m[l + 1] * ((f_m[l] + xi * hg_m[l]) + w)
            v_m[j, l + 1] = w if j == 0 else w - v_m[j - 1, l + 1]
            return w
        loop(L, 8, down_m, eta)

        xi_h, w_h, eta_h = join(const_h, own_h, (fp_h, gp_h))
        v_h[L + 1] = eta_h if j == 0 else eta_h - v_h[L + 1]

        def down_h(k, w):
            l = L - 1 - k
            w = m_h[l + 1] * ((f_h[l] + xi_h * hg_h[l]) + w)
            v_h[l + 1] = w if j == 0 else w - v_h[l + 1]
            return w
        loop(L, 8, down_h, eta_h)

    def apply_k(j):
        last = j == STEPS - 1

        def body(l):
            a = v_m[j, l + 1]
            b = v_h[l + 1]
            u_m[j, l + 1] = d_m[l] * a - beside(a, b) - 2.0 * (v_m[j, l] + v_m[j, l + 2])
            if not last:
                u_h[l] = mask_h * (d_h[l] * b - beside(b, a) - 2.0 * (v_h[l] + v_h[l + 2]))

        def end(l):
            a = v_m[j, l + 1]
            u_m[j, l + 1] = d_m[l] * a - beside(a, v_h[l + 1]) - 2.0 * (v_m[j, l] + v_m[j, l + 2])
        each(L, 4, body)
        if not last:
            end(L)

    def again_k(j):
        def body(l):
            a = u_m[j, l + 1]
            r_m[l] = d_m[l] * a - beside(a, u_h[l]) - 2.0 * (u_m[j, l] + u_m[j, l + 2])
        each(L, 4, body)

    def fold(acc):
        row = jnp.sum(acc, axis=0, keepdims=True)
        total = row[:, :128]
        for n in range(1, Y // 128):
            total = total + row[:, n * 128:(n + 1) * 128]
        return total

    def dots(j):
        def body(l, carry):
            u = u_m[j, l + 1]
            out = [carry[0] + v_m[j, l + 1] * s_m[l + 1]]
            for i in range(j + 1):
                out.append(carry[i + 1] + u * u_m[i, l + 1])
            return tuple(out)
        sums = loop(L, 4, body, (zero,) * (j + 2))
        gram[len(PAIRS) + j:len(PAIRS) + j + 1] = fold(sums[0])
        for i in range(j + 1):
            n = ROW[i, j]
            gram[n:n + 1] = fold(sums[i + 1])

    def side_terms():
        for copy in late:
            copy.wait_recv()

        def put_oh(l, x):
            o_h[l] = x * mask_h
        unpack(halo_in.at[0, 2], halo_in.at[1, 2], put_oh)

        def body(l):
            a = s_m[l + 1]
            ks[l] = d_m[l] * a - beside(a, s_h[l]) - 2.0 * (s_m[l] + s_m[l + 2])
            b = o_m[l + 1]
            ko = d_m[l] * b - beside(b, o_h[l]) - 2.0 * (o_m[l] + o_m[l + 2])
            data[l] = 2.0 * b * ko
        each(L, 4, body)

    finish(0, own_m, own_h, fp_m, gp_m, fp_h, gp_h)
    apply_k(0)
    for j in range(1, STEPS):
        n = j - 1
        again_k(j - 1)
        pack(lambda l: r_m[l], xs_out.at[n, 0], xs_out.at[n, 1])
        rows = [
            post(xs_out.at[n, 0], xs_in.at[n, 0], {"tile": nxt}),
            post(xs_out.at[n, 1], xs_in.at[n, 1], {"tile": prv}),
        ]
        own_m = passes(lambda l: r_m[l], m_m, f_m)
        pl_out[n, 0] = own_m[0]
        pl_out[n, 1] = own_m[1]
        planes = [
            post(pl_out.at[n], pl_in.at[n, 0], {"tile": nxt, "level": other}),
            post(pl_out.at[n], pl_in.at[n, 1], {"tile": prv, "level": other}),
            post(pl_out.at[n], pl_in.at[n, 2], {"level": other}),
        ]
        dots(j - 1)
        if j == 1:
            side_terms()
        for copy in rows:
            copy.wait_recv()

        def put_rh(l, x):
            r_h[l] = x * mask_h
        unpack(xs_in.at[n, 0], xs_in.at[n, 1], put_rh)
        own_h = passes(lambda l: r_h[l], m_h, f_h)
        for copy in planes:
            copy.wait_recv()
        fp_h = mask_h * jnp.where(sub >= 4, pl_in[n, 0, 0], pl_in[n, 1, 0])
        gp_h = mask_h * jnp.where(sub >= 4, pl_in[n, 0, 1], pl_in[n, 1, 1])
        finish(j, own_m, own_h, pl_in[n, 2, 0], pl_in[n, 2, 1], fp_h, gp_h)
        apply_k(j)
    for n in range(len(PAIRS) + STEPS, N_ROWS):
        gram[n:n + 1] = jnp.zeros((1, 128), F32)
    dots(STEPS - 1)

    red_a[grp] = gram[...]
    copies = [send(gram, red_a.at[grp], sa_sem.at[g], ra_sem.at[grp], dev) for g, dev in a_peers]
    started.extend(copies)
    for g, dev in a_peers:
        pltpu.make_async_remote_copy(
            src_ref=gram, dst_ref=red_a.at[g], send_sem=sa_sem.at[g], recv_sem=ra_sem.at[g],
            device_id=dev, device_id_type=MESH).wait_recv()
    red_b[zc] = sum((red_a[g] for g in range(1, n_a)), red_a[0])
    for g, dev in b_peers:
        started.append(send(red_b.at[zc], red_b.at[zc], sb_sem.at[g], rb_sem.at[zc], dev))
    for g, dev in b_peers:
        pltpu.make_async_remote_copy(
            src_ref=red_b.at[zc], dst_ref=red_b.at[g], send_sem=sb_sem.at[g], recv_sem=rb_sem.at[g],
            device_id=dev, device_id_type=MESH).wait_recv()
    total = sum((red_b[g] for g in range(1, z_chips)), red_b[0])
    total = jnp.broadcast_to(jnp.sum(total, axis=1, keepdims=True), (N_ROWS, Y))

    a = {}
    for (i, j), n in ROW.items():
        a[i, j] = total[n:n + 1]
    c = [total[len(PAIRS) + j:len(PAIRS) + j + 1] for j in range(STEPS)]
    pivot = []
    ratio = {}
    for j in range(STEPS):
        pivot.append(1.0 / a[j, j])
        for i in range(j + 1, STEPS):
            ratio[j, i] = a[j, i] * pivot[j]
        for i in range(j + 1, STEPS):
            c[i] = c[i] - ratio[j, i] * c[j]
            for k in range(i, STEPS):
                a[i, k] = a[i, k] - ratio[j, i] * a[j, k]
    for j in range(STEPS - 1, -1, -1):
        c[j] = c[j] * pivot[j]
        for i in range(j + 1, STEPS):
            c[j] = c[j] - ratio[j, i] * c[i]
    c = [jnp.broadcast_to(x, (8, Y)) for x in c]

    def term(l):
        x = c[0] * v_m[0, l + 1]
        kx = c[0] * u_m[0, l + 1]
        for j in range(1, STEPS):
            x = x + c[j] * v_m[j, l + 1]
            kx = kx + c[j] * u_m[j, l + 1]
        return x * ks[l] + kx * s_m[l + 1]

    low = lane_h < 64
    H = L // 2

    def fill(l):
        top, bot = term(l), term(l + H)
        for q in range(Y // 128):
            p, b = top[:, q * 128:(q + 1) * 128], bot[:, q * 128:(q + 1) * 128]
            rs_out[2 * q, l] = jnp.where(low, p, pltpu.roll(b, 64, 1))
            rs_out[2 * q + 1, l] = jnp.where(low, pltpu.roll(p, 64, 1), b)
    each(H, 2, fill)
    for g, dev in p_peers:
        started.append(send(rs_out.at[g], rs_in.at[probe], sp_sem.at[g], rp_sem.at[probe], dev))

    odd = lax.rem(probe, 2) == 1
    cols = pl.ds(pl.multiple_of((probe // 2) * 128, 128), 128)
    keep = jnp.where(odd, jnp.where(low, 0, 1), jnp.where(low, 1, 0)) == 1

    def mine(ref, l, k):
        p, b = ref[l, :, cols], ref[k, :, cols]
        at_top = jnp.where(keep, p, pltpu.roll(p, 64, 1))
        at_bot = jnp.where(keep, b, pltpu.roll(b, 64, 1))
        return jnp.where(low, at_top, at_bot)

    for g, dev in p_peers:
        pltpu.make_async_remote_copy(
            src_ref=rs_out.at[g], dst_ref=rs_in.at[g], send_sem=sp_sem.at[g], recv_sem=rp_sem.at[g],
            device_id=dev, device_id_type=MESH).wait_recv()

    def write(l):
        acc = rs_out[probe, l]
        for g, _ in p_peers:
            acc = acc + rs_in[g, l]
        kap = mine(kap_v, src(l), src(l + H))
        res = kap * (acc * (1.0 / probes) - mine(data, l, l + H))
        out_ref[src(l)] = res[:, :64]
        out_ref[src(l + H)] = pltpu.roll(res, 64, 1)[:, :64]
    each(H, 2, write)
    for copy in started:
        copy.wait_send()


def solution(mesh):
    probes, tiles, levels = (mesh.shape[a] for a in ("probe", "tile", "level"))
    x_chips = min(X_CHIPS, tiles)
    z_chips = tiles // x_chips

    def step(bits, kap, obs):
        _, L, rows, Y = bits.shape
        dims = (probes, tiles, levels, x_chips, L, Y)
        vm = lambda *lead: pltpu.VMEM((*lead, 8, Y), F32)
        dma = lambda n: pltpu.SemaphoreType.DMA((n,))
        G = L // 4
        scratch = [
            pltpu.VMEM((L, 8, Y), jnp.int32), vm(L), vm(L),
            vm(L + 2), vm(L), vm(L + 1), vm(L), vm(L + 2), vm(L),
            vm(L + 1), vm(L + 1), vm(L), vm(L),
            vm(STEPS, L + 3), vm(L + 2), vm(STEPS, L + 2), vm(L), vm(L), vm(L), vm(L), vm(L), vm(L), vm(L),
            vm(2, 3, G), vm(2, 3, G), vm(STEPS - 1, 2, G), vm(STEPS - 1, 2, G),
            vm(7), vm(7), vm(4), vm(4),
            vm(STEPS - 1, 2), vm(STEPS - 1, 3, 2),
            pltpu.VMEM((N_ROWS, 128), F32),
            pltpu.VMEM((levels * x_chips, N_ROWS, 128), F32),
            pltpu.VMEM((z_chips, N_ROWS, 128), F32),
            pltpu.VMEM((probes, L // 2, 8, 128), F32),
            pltpu.VMEM((probes, L // 2, 8, 128), F32),
            dma(3), dma(21), dma(21),
            dma(levels * x_chips), dma(levels * x_chips), dma(z_chips), dma(z_chips), dma(probes), dma(probes),
        ]
        return pl.pallas_call(
            functools.partial(kernel, dims),
            out_shape=jax.ShapeDtypeStruct((L, rows, Y // probes), F32),
            in_specs=[pl.BlockSpec(memory_space=pl.ANY)] * 3,
            out_specs=pl.BlockSpec(memory_space=pltpu.VMEM),
            scratch_shapes=scratch,
            compiler_params=pltpu.CompilerParams(collective_id=0, has_side_effects=True),
        )(bits, kap, obs)

    return jax.shard_map(
        step,
        mesh=mesh,
        in_specs=(P("probe", "level", "tile", None), P("level", "tile", None), P("level", "tile", None)),
        out_specs=P("level", "tile", "probe"),
        check_vma=False,
    )
```

time: 1670 us -> 64.7 us (0.04)
  blocking collectives: 1120 us -> 0 us
  waiting for transfers between devices: 323 us -> 0 us
  starting transfers between devices: 109 us -> 0 us
  Pallas kernels: 0 us -> 63 us
  local copies, waits for them, and re-layouts: 52.3 us -> 1.57 us
  other arithmetic: 41.6 us -> 0 us
  between operations: 23.8 us -> 0.01 us
    psum x7 -> x0, blocking collectives: 1060 us -> none  [the longest x4 607 us: precond_total(): return lax.psum(local_dots(residual, precond), ('tile', 'level'))]
    unnamed x2 -> x0, waiting for transfers between devices: 276 us -> none
    ppermute x40 -> x0, starting transfers between devices: 100 us -> none  [the longest x20 74.2 us: with_halo(): lax.ppermute(tail, axis, [(i, (i + 1) % count) for i in range(ends)])]
    pallas_call x0 -> x1, Pallas kernels: none -> 63 us  [step(): pl.pallas_call(functools.partial(kernel, dims), out_shape=jax.ShapeDtypeS...]
    all_to_all x7 -> x0, blocking collectives: 62.5 us -> none  [the longest x4 32 us: solve_columns(): lax.all_to_all(solved, 'level', split_axis=1, concat_axis=3, tiled=True)]
    ppermute x40 -> x0, waiting for transfers between devices: 40.6 us -> none  [the longest x20 32.6 us: with_halo(): lax.ppermute(head, axis, [((i + 1) % count, i) for i in range(ends)])]
    unnamed x66 -> x1, local copies, waits for them, and re-layouts: 33.4 us -> 1.57 us
  transfers between devices with their start and end apart: 43 -> 0, of which waited for: 18 -> 0; matrix products, arithmetic and copies ran while one was open for 1% -> 0% of each run, Pallas kernels for 0% -> 0%
where the time goes in v1:
time: 64.7 us; the launch traced here: 64.6 us
  Pallas kernels  63 us (97%)
  local copies, waits for them, and re-layouts  1.57 us (2%)
    pallas_call x1, Pallas kernels, step(): pl.pallas_call(functools.partial(kernel, dims), out_shape=jax.ShapeDtypeS...  63 us
    unnamed x1, local copies, waits for them, and re-layouts  1.57 us

profile of v1, /device:TPU:1, one launch (start us, length us, event | category | flops | bytes accessed | tf_op | source)
XLA Modules:
  0.0 64.6 jit_solution(9853738918625299385)
XLA Ops:
  0.0 63.0 %shard_map.37 = f32[32,8,64]{2,1,0:T(8,128)} custom-call(s32[1,32,8,256]{3,2,1,0:T(8,128)} %bits_hbm.1, f32[32,8,256]{2,1,0:T(8,128)} %kap_hbm.1, f32[32,8,256]{2,1,0:T(8,128)} %obs_hbm.1), custom_call_target="tpu_custom_call" | custom-call | tf_op jit(solution)/shard_map/pallas_call | solution.py:501
  63.0 1.6 %copy.5 = f32[32,8,64]{2,1,0:T(8,128)} copy(f32[32,8,64]{2,1,0:T(8,128)} %shard_map.37) | data formatting | bytes 131072

commit v2 on v1

v2 whole, which is shorter than its diff:
```python
import functools

import jax
import jax.numpy as jnp
from jax import lax
from jax.experimental import pallas as pl
from jax.experimental.pallas import tpu as pltpu
from jax.sharding import PartitionSpec as P

MESH = pl.DeviceIdType.MESH
STEPS = 4
F32 = jnp.float32
X_CHIPS = 4

PAIRS = [(i, j) for j in range(STEPS) for i in range(j + 1)]
ROW = {pair: n for n, pair in enumerate(PAIRS)}
N_ROWS = 16


def kernel(
    dims,
    bits_hbm, kap_hbm, obs_hbm, out_ref,
    bits_v, kap_v, obs_v,
    s_m, s_h, d_m, d_h, o_m, o_h,
    m_m, m_h, hg_m, hg_h,
    v_m, v_h, u_m, u_h, r_m, r_h, f_m, f_h, ks,
    halo_out, halo_in, xs_out, xs_in,
    first_out, first_in, pl_out, pl_in,
    gram, red_out, red_a, red_b, t_out, t_in, kap_q, sub_q, data,
    in_sem, send_sem, recv_sem,
):
    probes, tiles, levels, x_chips, L, Y = dims
    z_chips = tiles // x_chips
    H = L // 2
    probe = lax.axis_index("probe")
    tile = lax.axis_index("tile")
    half = lax.axis_index("level")
    zc = tile // x_chips
    xc = tile % x_chips
    nxt = lax.rem(tile + 1, tiles)
    prv = lax.rem(tile + tiles - 1, tiles)
    other = 1 - half
    n_a = probes * levels * x_chips
    spot = (probe * levels + half) * x_chips + xc

    loads = [
        pltpu.make_async_copy(kap_hbm, kap_v, in_sem.at[0]),
        pltpu.make_async_copy(bits_hbm.at[0], bits_v, in_sem.at[1]),
        pltpu.make_async_copy(obs_hbm, obs_v, in_sem.at[2]),
    ]
    for copy in loads:
        copy.start()

    a_peers = []
    for k in range(1, n_a):
        g = lax.rem(spot + k, n_a)
        a_peers.append({
            "probe": g // (levels * x_chips),
            "tile": zc * x_chips + g % x_chips,
            "level": (g // x_chips) % levels,
        })
    b_peers = [{"tile": lax.rem(zc + k, z_chips) * x_chips + xc} for k in range(1, z_chips)]
    p_peers = [lax.rem(probe + k, probes) for k in range(1, probes)]

    barrier = pltpu.get_barrier_semaphore()
    greet = [{"tile": nxt}, {"tile": prv}, {"tile": nxt, "level": other}, {"tile": prv, "level": other}]
    greet += a_peers + b_peers
    for dev in greet:
        pl.semaphore_signal(barrier, inc=1, device_id=dev, device_id_type=MESH)

    sub = lax.broadcasted_iota(jnp.int32, (8, Y), 0)
    lane_h = lax.broadcasted_iota(jnp.int32, (8, 128), 1)
    sub_h = lax.broadcasted_iota(jnp.int32, (8, 128), 0)
    has_next = (tile < tiles - 1).astype(F32)
    has_prev = (tile > 0).astype(F32)
    mask_h = jnp.where(sub < 2, has_next, jnp.where(sub >= 6, has_prev, 0.0))
    zero = jnp.zeros((8, Y), F32)

    def src(l):
        return half * (L - 1) + (1 - 2 * half) * l

    def send(src_ref, dst_ref, ssem, rsem, dev):
        copy = pltpu.make_async_remote_copy(
            src_ref=src_ref, dst_ref=dst_ref, send_sem=ssem, recv_sem=rsem,
            device_id=dev, device_id_type=MESH)
        copy.start()
        return copy

    started = []
    counter = [0]

    def post(src_ref, dst_ref, dev):
        n = counter[0]
        counter[0] += 1
        copy = send(src_ref, dst_ref, send_sem.at[n], recv_sem.at[n], dev)
        started.append(copy)
        return copy

    def loop(n, chunk, body, init=0):
        chunk = min(chunk, n)

        def step(b, carry):
            for k in range(chunk):
                carry = body(b * chunk + k, carry)
            return carry

        return lax.fori_loop(0, n // chunk, step, init)

    def each(n, chunk, body):
        def step(l, carry):
            body(l)
            return carry
        loop(n, chunk, step)

    def pack_rows(rows, g, up_ref, dn_ref):
        up = rows[3]
        dn = pltpu.roll(rows[3], 6, 0)
        for k in (2, 1, 0):
            up = jnp.where(sub < 2 * k + 2, pltpu.roll(rows[k], 2 * k + 2, 0), up)
            dn = jnp.where(sub < 2 * k + 2, pltpu.roll(rows[k], 2 * k, 0) if k else rows[k], dn)
        up_ref[g] = up
        dn_ref[g] = dn

    def pack(put, up_ref, dn_ref):
        each(L // 4, 2, lambda g: pack_rows([put(4 * g + k) for k in range(4)], g, up_ref, dn_ref))

    def unpack(a_ref, b_ref, write):
        def body(g):
            a = a_ref[g]
            b = b_ref[g]
            for k in range(4):
                ra = pltpu.roll(a, 6 - 2 * k, 0) if k < 3 else a
                rb = pltpu.roll(b, 8 - 2 * k, 0) if k else b
                write(4 * g + k, jnp.where(sub >= 4, ra, rb))
        each(L // 4, 2, body)

    first_lane = lane_h == 0
    last_lane = lane_h == 127

    def sides(a):
        parts = [a[:, n * 128:(n + 1) * 128] for n in range(Y // 128)]
        right = [pltpu.roll(x, 1, 1) for x in parts]
        left = [pltpu.roll(x, 127, 1) for x in parts]
        out = []
        for n in range(len(parts)):
            before = jnp.where(first_lane, right[n - 1] if n else 0.0, right[n])
            after = jnp.where(last_lane, left[n + 1] if n + 1 < len(parts) else 0.0, left[n])
            out.append(before + after)
        return jnp.concatenate(out, axis=1)

    def beside(a, b):
        up = jnp.where(sub == 0, pltpu.roll(b, 1, 0), pltpu.roll(a, 1, 0))
        dn = jnp.where(sub == 7, pltpu.roll(b, 7, 0), pltpu.roll(a, 7, 0))
        return (up + dn) + sides(a)

    def factor(d_ref, m_ref, hg_ref):
        m_ref[0] = zero

        def up(l, m):
            m = 2.0 / (d_ref[l] - 2.0 * m)
            m_ref[l + 1] = m
            return m
        last = loop(L, 8, up, zero)

        def down(k, h):
            l = L - 1 - k
            h = m_ref[l + 1] * h
            hg_ref[l] = h
            return h
        loop(L, 8, down, zero + 1.0)

        def again(l, g):
            g = 0.5 * hg_ref[l] + m_ref[l] * g
            hg_ref[l] = g
            return g
        return last, loop(L, 8, again, zero)

    def passes(read, m_ref, f_ref):
        def fwd(l, f):
            f = 0.5 * read(l) + m_ref[l] * f
            f_ref[l] = f
            return f
        first = loop(L, 16, fwd, zero)

        def back(k, y):
            l = L - 1 - k
            y = m_ref[l + 1] * (f_ref[l] + y)
            f_ref[l] = y
            return y
        loop(L, 16, back, zero)

        def again(l, g):
            g = 0.5 * f_ref[l] + m_ref[l] * g
            f_ref[l] = g
            return g
        return first, loop(L, 16, again, zero)

    def join(const, own, far):
        mo, ho, mp, hp, inv = const
        (fo, go), (fp, gp) = own, far
        x = mo * (fo + mp * fp) * inv
        xi = mp * (fp + mo * fo) * inv
        g = go + xi * ho
        gf = gp + x * hp
        w = mo * (g + mp * gf) * inv
        eta = mp * (gf + mo * g) * inv
        return xi, w, eta

    def finish_m(j, const, own, far, dp):
        xi, w, eta = join(const, own, far)
        beyond = 0.5 * (dp * eta - xi) - w
        v_m[j, L + 1] = eta if j == 0 else eta - v_m[j - 1, L + 1]
        v_m[j, L + 2] = beyond if j == 0 else beyond - v_m[j - 1, L + 2]

        def down(k, w):
            l = L - 1 - k
            w = m_m[l + 1] * ((f_m[l] + xi * hg_m[l]) + w)
            v_m[j, l + 1] = w if j == 0 else w - v_m[j - 1, l + 1]
            return w
        loop(L, 16, down, eta)

    def finish_h(j, const, own, far):
        xi, w, eta = join(const, own, far)
        v_h[L + 1] = eta if j == 0 else eta - v_h[L + 1]

        def down(k, w):
            l = L - 1 - k
            w = m_h[l + 1] * ((f_h[l] + xi * hg_h[l]) + w)
            v_h[l + 1] = w if j == 0 else w - v_h[l + 1]
            return w
        loop(L, 16, down, eta)

    def inner_k(j):
        def body(l):
            a = v_m[j, l + 1]
            rows = jnp.where(sub == 0, 0.0, pltpu.roll(a, 1, 0)) + jnp.where(sub == 7, 0.0, pltpu.roll(a, 7, 0))
            u_m[j, l + 1] = (d_m[l] * a - (rows + sides(a))) - 2.0 * (v_m[j, l] + v_m[j, l + 2])
        each(L, 8, body)
        if j < STEPS - 1:
            body(L)

    def outer_k(j):
        def fix(l, b):
            add = jnp.where(sub == 0, pltpu.roll(b, 1, 0), jnp.where(sub == 7, pltpu.roll(b, 7, 0), 0.0))
            u_m[j, l + 1] = u_m[j, l + 1] - add

        def body(l):
            b = v_h[l + 1]
            fix(l, b)
            if j < STEPS - 1:
                u = (d_h[l] * b - beside(b, v_m[j, l + 1])) - 2.0 * (v_h[l] + v_h[l + 2])
                u_h[l] = mask_h * u
        each(L, 8, body)
        if j < STEPS - 1:
            fix(L, v_h[L + 1])

    def again_k(j, l):
        a = u_m[j, l + 1]
        r = (d_m[l] * a - beside(a, u_h[l])) - 2.0 * (u_m[j, l] + u_m[j, l + 2])
        r_m[l] = r
        return r

    def fold(acc):
        row = jnp.sum(acc, axis=0, keepdims=True)
        total = row[:, :128]
        for n in range(1, Y // 128):
            total = total + row[:, n * 128:(n + 1) * 128]
        return total

    def dots(j):
        def body(l, carry):
            u = u_m[j, l + 1]
            out = [carry[0] + v_m[j, l + 1] * s_m[l + 1]]
            for i in range(j + 1):
                out.append(carry[i + 1] + u * u_m[i, l + 1])
            return tuple(out)
        sums = loop(L, 8, body, (zero,) * (j + 2))
        gram[len(PAIRS) + j:len(PAIRS) + j + 1] = fold(sums[0])
        for i in range(j + 1):
            n = ROW[i, j]
            gram[n:n + 1] = fold(sums[i + 1])

    low = lane_h < 64

    def quarter(q, top, bot):
        n = q // 2
        p, b = top[:, n * 128:(n + 1) * 128], bot[:, n * 128:(n + 1) * 128]
        if q % 2 == 0:
            return jnp.where(low, p, pltpu.roll(b, 64, 1))
        return jnp.where(low, pltpu.roll(p, 64, 1), b)

    def fill_t(j):
        def body(l):
            top = v_m[j, l + 1] * ks[l] + u_m[j, l + 1] * s_m[l + 1]
            k = l + H
            bot = v_m[j, k + 1] * ks[k] + u_m[j, k + 1] * s_m[k + 1]
            for q in range(probes):
                t_out[j, q, l] = quarter(q, top, bot)
            t_in[j, probe, l] = t_out[j, probe, l]
        each(H, 2, body)

    trace_parts = []

    def send_t(j):
        for g in p_peers:
            trace_parts.append(post(t_out.at[j, g], t_in.at[j, probe], {"probe": g}))

    loads[0].wait()

    def put_d(l):
        d = kap_v[src(l)] + 8.0
        d_m[l] = d
        return d
    pack(put_d, halo_out.at[0, 0], halo_out.at[0, 1])
    pl.semaphore_wait(barrier, len(greet))
    halo_d = [
        post(halo_out.at[0, 0], halo_in.at[0, 0], {"tile": nxt}),
        post(halo_out.at[0, 1], halo_in.at[0, 1], {"tile": prv}),
    ]
    loads[1].wait()

    def put_s(l):
        s = (2 * bits_v[src(l)] - 1).astype(F32)
        s_m[l + 1] = s
        return s
    pack(put_s, halo_out.at[1, 0], halo_out.at[1, 1])
    halo_s = [
        post(halo_out.at[1, 0], halo_in.at[1, 0], {"tile": nxt}),
        post(halo_out.at[1, 1], halo_in.at[1, 1], {"tile": prv}),
    ]
    s_m[0] = zero
    o_m[0] = zero
    for j in range(STEPS):
        v_m[j, 0] = zero
        u_m[j, 0] = zero
    v_h[0] = zero

    mo_m, ho_m = factor(d_m, m_m, hg_m)
    own_m = passes(lambda l: s_m[l + 1], m_m, f_m)
    loads[2].wait()
    for n, plane in enumerate((mo_m, ho_m, own_m[0], own_m[1], d_m[L - 1], s_m[L], obs_v[src(L - 1)])):
        first_out[n] = plane
    far = [
        post(first_out.at[pl.ds(0, 4)], first_in.at[0, pl.ds(0, 4)], {"tile": nxt, "level": other}),
        post(first_out.at[pl.ds(0, 4)], first_in.at[1, pl.ds(0, 4)], {"tile": prv, "level": other}),
        post(first_out, first_in.at[2], {"level": other}),
    ]

    def put_o(l):
        o = obs_v[src(l)]
        o_m[l + 1] = o
        return o
    pack(put_o, halo_out.at[2, 0], halo_out.at[2, 1])
    halo_o = [
        post(halo_out.at[2, 0], halo_in.at[2, 0], {"tile": nxt}),
        post(halo_out.at[2, 1], halo_in.at[2, 1], {"tile": prv}),
    ]

    for copy in halo_d:
        copy.wait_recv()

    def put_dh(l, x):
        d_h[l] = jnp.where(mask_h > 0.0, x, 8.0)
    unpack(halo_in.at[0, 0], halo_in.at[0, 1], put_dh)
    mo_h, ho_h = factor(d_h, m_h, hg_h)

    far[2].wait_recv()
    mp_m, hp_m, fp_m, gp_m, dp_m = (first_in[2, n] for n in range(5))
    d_m[L] = dp_m
    s_m[L + 1] = first_in[2, 5]
    o_m[L + 1] = first_in[2, 6]
    const_m = (mo_m, ho_m, mp_m, hp_m, 1.0 / (1.0 - mo_m * mp_m))
    finish_m(0, const_m, own_m, (fp_m, gp_m), dp_m)
    inner_k(0)

    for copy in halo_s:
        copy.wait_recv()

    def put_sh(l, x):
        s_h[l] = x * mask_h
    unpack(halo_in.at[1, 0], halo_in.at[1, 1], put_sh)
    own_h = passes(lambda l: s_h[l], m_h, f_h)
    for copy in far[:2]:
        copy.wait_recv()

    def beyond_rows(a, b):
        return jnp.where(sub >= 4, a, b)
    mp_h, hp_h, fp_h, gp_h = (beyond_rows(first_in[0, n], first_in[1, n]) for n in range(4))
    const_h = (mo_h, ho_h, mp_h, hp_h, 1.0 / (1.0 - mo_h * mp_h))
    finish_h(0, const_h, own_h, (mask_h * fp_h, mask_h * gp_h))
    outer_k(0)

    odd = lax.rem(probe, 2) == 1
    upper = probe // 2 == 1

    def mine(top, bot):
        out = [jnp.where(odd, quarter(2 * n + 1, top, bot), quarter(2 * n, top, bot)) for n in range(Y // 128)]
        return jnp.where(upper, out[1], out[0])

    def side_terms():
        for copy in halo_o:
            copy.wait_recv()

        def put_oh(l, x):
            o_h[l] = x * mask_h
        unpack(halo_in.at[2, 0], halo_in.at[2, 1], put_oh)

        def body(l):
            a = s_m[l + 1]
            ks[l] = (d_m[l] * a - beside(a, s_h[l])) - 2.0 * (s_m[l] + s_m[l + 2])
            b = o_m[l + 1]
            ko = (d_m[l] * b - beside(b, o_h[l])) - 2.0 * (o_m[l] + o_m[l + 2])
            data[l] = kap_v[src(l)] * (2.0 * b * ko)
        each(L, 4, body)

    def quarters():
        def body(l):
            kap_q[l] = mine(kap_v[src(l)], kap_v[src(l + H)]) * (1.0 / probes)
            sub_q[l] = mine(data[l], data[l + H])
        each(H, 2, body)

    for j in range(1, STEPS):
        n = j - 1
        pack(lambda l: again_k(j - 1, l), xs_out.at[n, 0], xs_out.at[n, 1])
        rows = [
            post(xs_out.at[n, 0], xs_in.at[n, 0], {"tile": nxt}),
            post(xs_out.at[n, 1], xs_in.at[n, 1], {"tile": prv}),
        ]
        own_m = passes(lambda l: r_m[l], m_m, f_m)
        pl_out[n, 0] = own_m[0]
        pl_out[n, 1] = own_m[1]
        planes = [
            post(pl_out.at[n], pl_in.at[n, 0], {"tile": nxt, "level": other}),
            post(pl_out.at[n], pl_in.at[n, 1], {"tile": prv, "level": other}),
            post(pl_out.at[n], pl_in.at[n, 2], {"level": other}),
        ]
        dots(j - 1)
        if j == 1:
            side_terms()
        if j == 2:
            quarters()
        fill_t(j - 1)
        planes[2].wait_recv()
        finish_m(j, const_m, own_m, (pl_in[n, 2, 0], pl_in[n, 2, 1]), dp_m)
        inner_k(j)
        for copy in rows:
            copy.wait_recv()

        def put_rh(l, x):
            r_h[l] = x * mask_h
        unpack(xs_in.at[n, 0], xs_in.at[n, 1], put_rh)
        own_h = passes(lambda l: r_h[l], m_h, f_h)
        for copy in planes[:2]:
            copy.wait_recv()
        send_t(j - 1)
        fp_h = mask_h * beyond_rows(pl_in[n, 0, 0], pl_in[n, 1, 0])
        gp_h = mask_h * beyond_rows(pl_in[n, 0, 1], pl_in[n, 1, 1])
        finish_h(j, const_h, own_h, (fp_h, gp_h))
        outer_k(j)
    for n in range(len(PAIRS) + STEPS, N_ROWS):
        gram[n:n + 1] = jnp.zeros((1, 128), F32)
    dots(STEPS - 1)

    wide = lax.broadcasted_iota(jnp.int32, (N_ROWS, 128), 1) == lax.broadcasted_iota(jnp.int32, (N_ROWS, 128), 0)
    each_sum = jnp.sum(gram[...], axis=1, keepdims=True)
    packed = jnp.sum(jnp.where(wide, each_sum, 0.0), axis=0, keepdims=True)
    red_out[...] = packed
    red_a[spot] = packed
    plane = [post(red_out, red_a.at[spot], dev) for dev in a_peers]
    fill_t(STEPS - 1)
    send_t(STEPS - 1)
    for copy in plane:
        copy.wait_recv()
    for p in range(probes):
        base = p * levels * x_chips
        part = red_a[base]
        for k in range(1, levels * x_chips):
            part = part + red_a[base + k]
        red_b[zc, p] = part
    line = [post(red_b.at[zc], red_b.at[zc], dev) for dev in b_peers]
    for copy in line:
        copy.wait_recv()
    total = None
    for p in range(probes):
        part = red_b[0, p]
        for k in range(1, z_chips):
            part = part + red_b[k, p]
        part = jnp.broadcast_to(part, (8, 128))
        total = part if p == 0 else jnp.where(sub_h == p, part, total)

    def column(n):
        return jnp.broadcast_to(total[:, n:n + 1], (8, 128))
    a = {pair: column(n) for pair, n in ROW.items()}
    c = [column(len(PAIRS) + j) for j in range(STEPS)]
    pivot = []
    ratio = {}
    for j in range(STEPS):
        pivot.append(1.0 / a[j, j])
        for i in range(j + 1, STEPS):
            ratio[j, i] = a[j, i] * pivot[j]
        for i in range(j + 1, STEPS):
            c[i] = c[i] - ratio[j, i] * c[j]
            for k in range(i, STEPS):
                a[i, k] = a[i, k] - ratio[j, i] * a[j, k]
    for j in range(STEPS - 1, -1, -1):
        c[j] = c[j] * pivot[j]
        for i in range(j + 1, STEPS):
            c[j] = c[j] - ratio[j, i] * c[i]
    weight = {(p, j): jnp.broadcast_to(c[j][p:p + 1], (8, 128)) for p in range(probes) for j in range(STEPS)}

    for copy in trace_parts:
        copy.wait_recv()

    def write(l):
        acc = None
        for j in range(STEPS):
            for p in range(probes):
                part = weight[p, j] * t_in[j, p, l]
                acc = part if acc is None else acc + part
        res = kap_q[l] * acc - sub_q[l]
        out_ref[src(l)] = res[:, :64]
        out_ref[src(l + H)] = pltpu.roll(res, 64, 1)[:, :64]
    each(H, 4, write)
    for copy in started:
        copy.wait_send()


def solution(mesh):
    probes, tiles, levels = (mesh.shape[a] for a in ("probe", "tile", "level"))
    x_chips = min(X_CHIPS, tiles)
    z_chips = tiles // x_chips

    def step(bits, kap, obs):
        _, L, rows, Y = bits.shape
        dims = (probes, tiles, levels, x_chips, L, Y)
        vm = lambda *lead: pltpu.VMEM((*lead, 8, Y), F32)
        dma = lambda n: pltpu.SemaphoreType.DMA((n,))
        G = L // 4
        n_sems = 9 + 5 * (STEPS - 1) + (probes * levels * x_chips - 1) + (z_chips - 1) + STEPS * (probes - 1)
        part = lambda *lead: pltpu.VMEM((*lead, L // 2, 8, 128), F32)
        scratch = [
            pltpu.VMEM((L, 8, Y), jnp.int32), vm(L), vm(L),
            vm(L + 2), vm(L), vm(L + 1), vm(L), vm(L + 2), vm(L),
            vm(L + 1), vm(L + 1), vm(L), vm(L),
            vm(STEPS, L + 3), vm(L + 2), vm(STEPS, L + 2), vm(L), vm(L), vm(L), vm(L), vm(L), vm(L),
            vm(3, 2, G), vm(3, 2, G), vm(STEPS - 1, 2, G), vm(STEPS - 1, 2, G),
            vm(7), vm(3, 7), vm(STEPS - 1, 2), vm(STEPS - 1, 3, 2),
            pltpu.VMEM((N_ROWS, 128), F32),
            pltpu.VMEM((1, 128), F32),
            pltpu.VMEM((probes * levels * x_chips, 1, 128), F32),
            pltpu.VMEM((z_chips, probes, 1, 128), F32),
            part(STEPS, probes), part(STEPS, probes), part(), part(), vm(L),
            dma(3), dma(n_sems), dma(n_sems),
        ]
        return pl.pallas_call(
            functools.partial(kernel, dims),
            out_shape=jax.ShapeDtypeStruct((L, rows, Y // probes), F32),
            in_specs=[pl.BlockSpec(memory_space=pl.ANY)] * 3,
            out_specs=pl.BlockSpec(memory_space=pltpu.VMEM),
            scratch_shapes=scratch,
            compiler_params=pltpu.CompilerParams(collective_id=0, has_side_effects=True),
        )(bits, kap, obs)

    return jax.shard_map(
        step,
        mesh=mesh,
        in_specs=(P("probe", "level", "tile", None), P("level", "tile", None), P("level", "tile", None)),
        out_specs=P("level", "tile", "probe"),
        check_vma=False,
    )
```

time: 64.7 us -> 54.4 us (0.84)
  Pallas kernels: 63 us -> 52.7 us
    pallas_call x1, Pallas kernels: 63 us -> 52.7 us  [step(): pl.pallas_call(functools.partial(kernel, dims), out_shape=jax.ShapeDtypeS...]
where the time goes in v2:
time: 54.4 us; the launch traced here: 54.3 us
  Pallas kernels  52.7 us (97%)
  local copies, waits for them, and re-layouts  1.57 us (3%)
    pallas_call x1, Pallas kernels, step(): pl.pallas_call(functools.partial(kernel, dims), out_shape=jax.ShapeDtypeS...  52.7 us
    unnamed x1, local copies, waits for them, and re-layouts  1.57 us

profile of v2, /device:TPU:1, one launch (start us, length us, event | category | flops | bytes accessed | tf_op | source)
XLA Modules:
  0.0 54.3 jit_solution(3163475613859089298)
XLA Ops:
  0.0 52.7 %shard_map.37 = f32[32,8,64]{2,1,0:T(8,128)} custom-call(s32[1,32,8,256]{3,2,1,0:T(8,128)} %bits_hbm.1, f32[32,8,256]{2,1,0:T(8,128)} %kap_hbm.1, f32[32,8,256]{2,1,0:T(8,128)} %obs_hbm.1), custom_call_target="tpu_custom_call" | custom-call | tf_op jit(solution)/shard_map/pallas_call | solution.py:555
  52.7 1.6 %copy.5 = f32[32,8,64]{2,1,0:T(8,128)} copy(f32[32,8,64]{2,1,0:T(8,128)} %shard_map.37) | data formatting | bytes 131072

commit v3 on v2

--- a/solution.py
+++ b/solution.py
@@ -22,10 +22,10 @@
     bits_hbm, kap_hbm, obs_hbm, out_ref,
     bits_v, kap_v, obs_v,
     s_m, s_h, d_m, d_h, o_m, o_h,
-    m_m, m_h, hg_m, hg_h,
-    v_m, v_h, u_m, u_h, r_m, r_h, f_m, f_h, ks,
+    m_m, m_h, hg_m, hg_h, al_m, be_m,
+    v_m, v_h, u_m, u_h, r_m, r_h, f_m, f_h, y_f, ks,
     halo_out, halo_in, xs_out, xs_in,
-    first_out, first_in, pl_out, pl_in,
+    first_out, first_in, side_out, side_in, pl_out, pl_in, ed_out, ed_in,
     gram, red_out, red_a, red_b, t_out, t_in, kap_q, sub_q, data,
     in_sem, send_sem, recv_sem,
 ):
@@ -36,7 +36,7 @@
     tile = lax.axis_index("tile")
     half = lax.axis_index("level")
     zc = tile // x_chips
-    xc = tile % x_chips
+    xc = tile - zc * x_chips
     nxt = lax.rem(tile + 1, tiles)
     prv = lax.rem(tile + tiles - 1, tiles)
     other = 1 - half
@@ -51,16 +51,12 @@
     for copy in loads:
         copy.start()
 
-    a_peers = []
-    for k in range(1, n_a):
-        g = lax.rem(spot + k, n_a)
-        a_peers.append({
-            "probe": g // (levels * x_chips),
-            "tile": zc * x_chips + g % x_chips,
-            "level": (g // x_chips) % levels,
-        })
-    b_peers = [{"tile": lax.rem(zc + k, z_chips) * x_chips + xc} for k in range(1, z_chips)]
-    p_peers = [lax.rem(probe + k, probes) for k in range(1, probes)]
+    near_p = [probe] + [lax.rem(probe + k, probes) for k in range(1, probes)]
+    near_x = [tile] + [tile - xc + lax.rem(xc + k, x_chips) for k in range(1, x_chips)]
+    near_h = [half, other]
+    a_peers = [{"probe": p, "tile": t, "level": h} for t in near_x for h in near_h for p in near_p][1:]
+    b_peers = [{"tile": lax.rem(tile + k * x_chips, tiles)} for k in range(1, z_chips)]
+    p_peers = near_p[1:]
 
     barrier = pltpu.get_barrier_semaphore()
     greet = [{"tile": nxt}, {"tile": prv}, {"tile": nxt, "level": other}, {"tile": prv, "level": other}]
@@ -175,7 +171,7 @@
             return g
         return last, loop(L, 8, again, zero)
 
-    def passes(read, m_ref, f_ref):
+    def solve(read, m_ref, f_ref, y_ref):
         def fwd(l, f):
             f = 0.5 * read(l) + m_ref[l] * f
             f_ref[l] = f
@@ -185,15 +181,26 @@
         def back(k, y):
             l = L - 1 - k
             y = m_ref[l + 1] * (f_ref[l] + y)
-            f_ref[l] = y
+            y_ref[l] = y
             return y
         loop(L, 16, back, zero)
+        return first
+
+    def passes(read, m_ref, f_ref):
+        first = solve(read, m_ref, f_ref, y_f)
 
         def again(l, g):
-            g = 0.5 * f_ref[l] + m_ref[l] * g
+            g = 0.5 * y_f[l] + m_ref[l] * g
             f_ref[l] = g
             return g
         return first, loop(L, 16, again, zero)
+
+    def edges(a, b):
+        inside = jnp.where(sub < 4, pltpu.roll(b, 2, 0), pltpu.roll(b, 6, 0))
+        return jnp.where((sub >= 2) & (sub < 6), inside, a)
+
+    def beyond(a, b):
+        return jnp.where(sub >= 4, a, b), jnp.where(sub >= 4, pltpu.roll(a, 2, 0), pltpu.roll(b, 6, 0))
 
     def join(const, own, far):
         mo, ho, mp, hp, inv = const
@@ -208,9 +215,9 @@
 
     def finish_m(j, const, own, far, dp):
         xi, w, eta = join(const, own, far)
-        beyond = 0.5 * (dp * eta - xi) - w
+        next_one = 0.5 * (dp * eta - xi) - w
         v_m[j, L + 1] = eta if j == 0 else eta - v_m[j - 1, L + 1]
-        v_m[j, L + 2] = beyond if j == 0 else beyond - v_m[j - 1, L + 2]
+        v_m[j, L + 2] = next_one if j == 0 else next_one - v_m[j - 1, L + 2]
 
         def down(k, w):
             l = L - 1 - k
@@ -317,6 +324,7 @@
         post(halo_out.at[0, 0], halo_in.at[0, 0], {"tile": nxt}),
         post(halo_out.at[0, 1], halo_in.at[0, 1], {"tile": prv}),
     ]
+    mo_m, ho_m = factor(d_m, m_m, hg_m)
     loads[1].wait()
 
     def put_s(l):
@@ -324,6 +332,17 @@
         s_m[l + 1] = s
         return s
     pack(put_s, halo_out.at[1, 0], halo_out.at[1, 1])
+    own_m = passes(lambda l: s_m[l + 1], m_m, f_m)
+    loads[2].wait()
+    side_out[0] = edges(mo_m, ho_m)
+    side_out[1] = edges(own_m[0], own_m[1])
+    for n, plane in enumerate((mo_m, ho_m, own_m[0], own_m[1], d_m[L - 1], s_m[L], obs_v[src(L - 1)])):
+        first_out[n] = plane
+    far = [
+        post(side_out, side_in.at[0], {"tile": nxt, "level": other}),
+        post(side_out, side_in.at[1], {"tile": prv, "level": other}),
+        post(first_out, first_in, {"level": other}),
+    ]
     halo_s = [
         post(halo_out.at[1, 0], halo_in.at[1, 0], {"tile": nxt}),
         post(halo_out.at[1, 1], halo_in.at[1, 1], {"tile": prv}),
@@ -335,17 +354,6 @@
         u_m[j, 0] = zero
     v_h[0] = zero
 
-    mo_m, ho_m = factor(d_m, m_m, hg_m)
-    own_m = passes(lambda l: s_m[l + 1], m_m, f_m)
-    loads[2].wait()
-    for n, plane in enumerate((mo_m, ho_m, own_m[0], own_m[1], d_m[L - 1], s_m[L], obs_v[src(L - 1)])):
-        first_out[n] = plane
-    far = [
-        post(first_out.at[pl.ds(0, 4)], first_in.at[0, pl.ds(0, 4)], {"tile": nxt, "level": other}),
-        post(first_out.at[pl.ds(0, 4)], first_in.at[1, pl.ds(0, 4)], {"tile": prv, "level": other}),
-        post(first_out, first_in.at[2], {"level": other}),
-    ]
-
     def put_o(l):
         o = obs_v[src(l)]
         o_m[l + 1] = o
@@ -356,6 +364,13 @@
         post(halo_out.at[2, 1], halo_in.at[2, 1], {"tile": prv}),
     ]
 
+    def weigh(k, x):
+        l = L - 1 - k
+        al_m[l] = x
+        return m_m[l] * x
+    loop(L, 16, weigh, zero + 0.5)
+    solve(lambda l: al_m[l], m_m, r_m, be_m)
+
     for copy in halo_d:
         copy.wait_recv()
 
@@ -365,10 +380,10 @@
     mo_h, ho_h = factor(d_h, m_h, hg_h)
 
     far[2].wait_recv()
-    mp_m, hp_m, fp_m, gp_m, dp_m = (first_in[2, n] for n in range(5))
+    mp_m, hp_m, fp_m, gp_m, dp_m = (first_in[n] for n in range(5))
     d_m[L] = dp_m
-    s_m[L + 1] = first_in[2, 5]
-    o_m[L + 1] = first_in[2, 6]
+    s_m[L + 1] = first_in[5]
+    o_m[L + 1] = first_in[6]
     const_m = (mo_m, ho_m, mp_m, hp_m, 1.0 / (1.0 - mo_m * mp_m))
     finish_m(0, const_m, own_m, (fp_m, gp_m), dp_m)
     inner_k(0)
@@ -383,9 +398,8 @@
     for copy in far[:2]:
         copy.wait_recv()
 
-    def beyond_rows(a, b):
-        return jnp.where(sub >= 4, a, b)
-    mp_h, hp_h, fp_h, gp_h = (beyond_rows(first_in[0, n], first_in[1, n]) for n in range(4))
+    mp_h, hp_h = beyond(side_in[0, 0], side_in[1, 0])
+    fp_h, gp_h = beyond(side_in[0, 1], side_in[1, 1])
     const_h = (mo_h, ho_h, mp_h, hp_h, 1.0 / (1.0 - mo_h * mp_h))
     finish_h(0, const_h, own_h, (mask_h * fp_h, mask_h * gp_h))
     outer_k(0)
@@ -421,19 +435,32 @@
 
     for j in range(1, STEPS):
         n = j - 1
-        pack(lambda l: again_k(j - 1, l), xs_out.at[n, 0], xs_out.at[n, 1])
+
+        def form(g, carry):
+            fo, go = carry
+            tiles_r = []
+            for k in range(4):
+                l = 4 * g + k
+                r = again_k(j - 1, l)
+                fo = fo + al_m[l] * r
+                go = go + be_m[l] * r
+                tiles_r.append(r)
+            pack_rows(tiles_r, g, xs_out.at[n, 0], xs_out.at[n, 1])
+            return fo, go
+        own_m = loop(L // 4, 2, form, (zero, zero))
+        ed_out[n] = edges(own_m[0], own_m[1])
+        pl_out[n, 0] = own_m[0]
+        pl_out[n, 1] = own_m[1]
+        planes = [
+            post(ed_out.at[n], ed_in.at[n, 0], {"tile": nxt, "level": other}),
+            post(ed_out.at[n], ed_in.at[n, 1], {"tile": prv, "level": other}),
+            post(pl_out.at[n], pl_in.at[n], {"level": other}),
+        ]
         rows = [
             post(xs_out.at[n, 0], xs_in.at[n, 0], {"tile": nxt}),
             post(xs_out.at[n, 1], xs_in.at[n, 1], {"tile": prv}),
         ]
-        own_m = passes(lambda l: r_m[l], m_m, f_m)
-        pl_out[n, 0] = own_m[0]
-        pl_out[n, 1] = own_m[1]
-        planes = [
-            post(pl_out.at[n], pl_in.at[n, 0], {"tile": nxt, "level": other}),
-            post(pl_out.at[n], pl_in.at[n, 1], {"tile": prv, "level": other}),
-            post(pl_out.at[n], pl_in.at[n, 2], {"level": other}),
-        ]
+        passes(lambda l: r_m[l], m_m, f_m)
         dots(j - 1)
         if j == 1:
             side_terms()
@@ -441,7 +468,7 @@
             quarters()
         fill_t(j - 1)
         planes[2].wait_recv()
-        finish_m(j, const_m, own_m, (pl_in[n, 2, 0], pl_in[n, 2, 1]), dp_m)
+        finish_m(j, const_m, own_m, (pl_in[n, 0], pl_in[n, 1]), dp_m)
         inner_k(j)
         for copy in rows:
             copy.wait_recv()
@@ -453,9 +480,8 @@
         for copy in planes[:2]:
             copy.wait_recv()
         send_t(j - 1)
-        fp_h = mask_h * beyond_rows(pl_in[n, 0, 0], pl_in[n, 1, 0])
-        gp_h = mask_h * beyond_rows(pl_in[n, 0, 1], pl_in[n, 1, 1])
-        finish_h(j, const_h, own_h, (fp_h, gp_h))
+        fp_h, gp_h = beyond(ed_in[n, 0], ed_in[n, 1])
+        finish_h(j, const_h, own_h, (mask_h * fp_h, mask_h * gp_h))
         outer_k(j)
     for n in range(len(PAIRS) + STEPS, N_ROWS):
         gram[n:n + 1] = jnp.zeros((1, 128), F32)
@@ -477,7 +503,10 @@
         for k in range(1, levels * x_chips):
             part = part + red_a[base + k]
         red_b[zc, p] = part
+    before = list(started)
     line = [post(red_b.at[zc], red_b.at[zc], dev) for dev in b_peers]
+    for copy in before:
+        copy.wait_send()
     for copy in line:
         copy.wait_recv()
     total = None
@@ -521,7 +550,7 @@
         out_ref[src(l)] = res[:, :64]
         out_ref[src(l + H)] = pltpu.roll(res, 64, 1)[:, :64]
     each(H, 4, write)
-    for copy in started:
+    for copy in line:
         copy.wait_send()
 
 
@@ -541,10 +570,11 @@
         scratch = [
             pltpu.VMEM((L, 8, Y), jnp.int32), vm(L), vm(L),
             vm(L + 2), vm(L), vm(L + 1), vm(L), vm(L + 2), vm(L),
-            vm(L + 1), vm(L + 1), vm(L), vm(L),
-            vm(STEPS, L + 3), vm(L + 2), vm(STEPS, L + 2), vm(L), vm(L), vm(L), vm(L), vm(L), vm(L),
+            vm(L + 1), vm(L + 1), vm(L), vm(L), vm(L), vm(L),
+            vm(STEPS, L + 3), vm(L + 2), vm(STEPS, L + 2), vm(L), vm(L), vm(L), vm(L), vm(L), vm(L), vm(L),
             vm(3, 2, G), vm(3, 2, G), vm(STEPS - 1, 2, G), vm(STEPS - 1, 2, G),
-            vm(7), vm(3, 7), vm(STEPS - 1, 2), vm(STEPS - 1, 3, 2),
+            vm(7), vm(7), vm(2), vm(2, 2),
+            vm(STEPS - 1, 2), vm(STEPS - 1, 2), vm(STEPS - 1), vm(STEPS - 1, 2),
             pltpu.VMEM((N_ROWS, 128), F32),
             pltpu.VMEM((1, 128), F32),
             pltpu.VMEM((probes * levels * x_chips, 1, 128), F32),

time: 54.4 us -> 50.9 us (0.936)
  Pallas kernels: 52.7 us -> 49.3 us
    pallas_call x1, Pallas kernels: 52.7 us -> 49.3 us  [step(): pl.pallas_call(functools.partial(kernel, dims), out_shape=jax.ShapeDtypeS...]
where the time goes in v3:
time: 50.9 us; the launch traced here: 50.8 us
  Pallas kernels  49.3 us (97%)
  local copies, waits for them, and re-layouts  1.57 us (3%)
    pallas_call x1, Pallas kernels, step(): pl.pallas_call(functools.partial(kernel, dims), out_shape=jax.ShapeDtypeS...  49.3 us
    unnamed x1, local copies, waits for them, and re-layouts  1.57 us

profile of v3, /device:TPU:1, one launch (start us, length us, event | category | flops | bytes accessed | tf_op | source)
XLA Modules:
  0.0 50.8 jit_solution(1288543445949143880)
XLA Ops:
  0.0 49.3 %shard_map.37 = f32[32,8,64]{2,1,0:T(8,128)} custom-call(s32[1,32,8,256]{3,2,1,0:T(8,128)} %bits_hbm.1, f32[32,8,256]{2,1,0:T(8,128)} %kap_hbm.1, f32[32,8,256]{2,1,0:T(8,128)} %obs_hbm.1), custom_call_target="tpu_custom_call" | custom-call | tf_op jit(solution)/shard_map/pallas_call | solution.py:585
  49.3 1.6 %copy.5 = f32[32,8,64]{2,1,0:T(8,128)} copy(f32[32,8,64]{2,1,0:T(8,128)} %shard_map.37) | data formatting | bytes 131072

commit v4 on v3

--- a/solution.py
+++ b/solution.py
@@ -27,7 +27,7 @@
     halo_out, halo_in, xs_out, xs_in,
     first_out, first_in, side_out, side_in, pl_out, pl_in, ed_out, ed_in,
     gram, red_out, red_a, red_b, t_out, t_in, kap_q, sub_q, data,
-    in_sem, send_sem, recv_sem,
+    in_sem, send_sem, recv_sem, here_sem,
 ):
     probes, tiles, levels, x_chips, L, Y = dims
     z_chips = tiles // x_chips
@@ -51,16 +51,23 @@
     for copy in loads:
         copy.start()
 
-    near_p = [probe] + [lax.rem(probe + k, probes) for k in range(1, probes)]
-    near_x = [tile] + [tile - xc + lax.rem(xc + k, x_chips) for k in range(1, x_chips)]
-    near_h = [half, other]
-    a_peers = [{"probe": p, "tile": t, "level": h} for t in near_x for h in near_h for p in near_p][1:]
-    b_peers = [{"tile": lax.rem(tile + k * x_chips, tiles)} for k in range(1, z_chips)]
-    p_peers = near_p[1:]
+    def around(n):
+        return sorted(range(1, n), key=lambda k: (-min(k, n - k), k))
+
+    near_p = [lax.rem(probe + k, probes) for k in around(probes)]
+    near_x = [tile - xc + lax.rem(xc + k, x_chips) for k in around(x_chips)]
+    a_peers = [{"probe": p, "tile": t, "level": h}
+               for t in near_x + [tile] for h in (other, half) for p in near_p + [probe]][:-1]
+    b_peers = [{"tile": lax.rem(tile + k * x_chips, tiles)} for k in around(z_chips)]
+    p_peers = near_p
+    z_beside = [{"tile": lax.rem(tile + x_chips, tiles)}, {"tile": lax.rem(tile + tiles - x_chips, tiles)}]
+    if z_chips == 1:
+        z_beside = []
 
     barrier = pltpu.get_barrier_semaphore()
-    greet = [{"tile": nxt}, {"tile": prv}, {"tile": nxt, "level": other}, {"tile": prv, "level": other}]
-    greet += a_peers + b_peers
+    greet = [{"tile": nxt}, {"tile": prv}, {"level": other},
+             {"tile": nxt, "level": other}, {"tile": prv, "level": other}]
+    greet += [{"probe": p} for p in p_peers] + z_beside
     for dev in greet:
         pl.semaphore_signal(barrier, inc=1, device_id=dev, device_id_type=MESH)
 
@@ -460,6 +467,8 @@
             post(xs_out.at[n, 0], xs_in.at[n, 0], {"tile": nxt}),
             post(xs_out.at[n, 1], xs_in.at[n, 1], {"tile": prv}),
         ]
+        for dev in z_beside:
+            pl.semaphore_signal(here_sem.at[n], inc=1, device_id=dev, device_id_type=MESH)
         passes(lambda l: r_m[l], m_m, f_m)
         dots(j - 1)
         if j == 1:
@@ -479,6 +488,8 @@
         own_h = passes(lambda l: r_h[l], m_h, f_h)
         for copy in planes[:2]:
             copy.wait_recv()
+        if z_beside:
+            pl.semaphore_wait(here_sem.at[n], len(z_beside))
         send_t(j - 1)
         fp_h, gp_h = beyond(ed_in[n, 0], ed_in[n, 1])
         finish_h(j, const_h, own_h, (mask_h * fp_h, mask_h * gp_h))
@@ -490,6 +501,8 @@
     wide = lax.broadcasted_iota(jnp.int32, (N_ROWS, 128), 1) == lax.broadcasted_iota(jnp.int32, (N_ROWS, 128), 0)
     each_sum = jnp.sum(gram[...], axis=1, keepdims=True)
     packed = jnp.sum(jnp.where(wide, each_sum, 0.0), axis=0, keepdims=True)
+    for copy in trace_parts[:probes - 1]:
+        copy.wait_recv()
     red_out[...] = packed
     red_a[spot] = packed
     plane = [post(red_out, red_a.at[spot], dev) for dev in a_peers]
@@ -537,7 +550,7 @@
             c[j] = c[j] - ratio[j, i] * c[i]
     weight = {(p, j): jnp.broadcast_to(c[j][p:p + 1], (8, 128)) for p in range(probes) for j in range(STEPS)}
 
-    for copy in trace_parts:
+    for copy in trace_parts[probes - 1:]:
         copy.wait_recv()
 
     def write(l):
@@ -580,11 +593,11 @@
             pltpu.VMEM((probes * levels * x_chips, 1, 128), F32),
             pltpu.VMEM((z_chips, probes, 1, 128), F32),
             part(STEPS, probes), part(STEPS, probes), part(), part(), vm(L),
-            dma(3), dma(n_sems), dma(n_sems),
+            dma(3), dma(n_sems), dma(n_sems), pltpu.SemaphoreType.REGULAR((STEPS - 1,)),
         ]
         return pl.pallas_call(
             functools.partial(kernel, dims),
-            out_shape=jax.ShapeDtypeStruct((L, rows, Y // probes), F32),
+            out_shape=pltpu.VMEM((L, rows, Y // probes), F32),
             in_specs=[pl.BlockSpec(memory_space=pl.ANY)] * 3,
             out_specs=pl.BlockSpec(memory_space=pltpu.VMEM),
             scratch_shapes=scratch,

time: 50.9 us -> 49 us (0.963)
  Pallas kernels: 49.3 us -> 48.3 us
  local copies, waits for them, and re-layouts: 1.57 us -> 0.66 us
    pallas_call x1, Pallas kernels: 49.3 us -> 48.3 us  [step(): pl.pallas_call(functools.partial(kernel, dims), out_shape=pltpu.VMEM((L,...]
    unnamed x1, local copies, waits for them, and re-layouts: 1.57 us -> 0.66 us
where the time goes in v4:
time: 49 us; the launch traced here: 48.9 us
  Pallas kernels  48.3 us (99%)
  local copies, waits for them, and re-layouts  0.66 us (1%)
    pallas_call x1, Pallas kernels, step(): pl.pallas_call(functools.partial(kernel, dims), out_shape=pltpu.VMEM((L,...  48.3 us

profile of v4, /device:TPU:1, one launch (start us, length us, event | category | flops | bytes accessed | tf_op | source)
XLA Modules:
  0.0 48.9 jit_solution(9706068405355901248)
XLA Ops:
  0.0 48.3 %shard_map.37 = f32[32,8,64]{2,1,0:T(8,128)S(1)} custom-call(s32[1,32,8,256]{3,2,1,0:T(8,128)} %bits_hbm.1, f32[32,8,256]{2,1,0:T(8,128)} %kap_hbm.1, f32[32,8,256]{2,1,0:T(8,128)} %obs_hbm.1), custom_call_target="tpu_custom_call" | custom-call | tf_op jit(solution)/shard_map/pallas_call | solution.py:598
  48.3 0.7 %copy.5 = f32[32,8,64]{2,1,0:T(8,128)} copy(f32[32,8,64]{2,1,0:T(8,128)S(1)} %shard_map.37) | data formatting | bytes 131072

commit v5 on v4

--- a/solution.py
+++ b/solution.py
@@ -23,7 +23,7 @@
     bits_v, kap_v, obs_v,
     s_m, s_h, d_m, d_h, o_m, o_h,
     m_m, m_h, hg_m, hg_h, al_m, be_m,
-    v_m, v_h, u_m, u_h, r_m, r_h, f_m, f_h, y_f, ks,
+    v_m, v_h, u_m, u_h, r_m, f_m, f_h, y_f, ks,
     halo_out, halo_in, xs_out, xs_in,
     first_out, first_in, side_out, side_in, pl_out, pl_in, ed_out, ed_in,
     gram, red_out, red_a, red_b, t_out, t_in, kap_q, sub_q, data,
@@ -127,15 +127,40 @@
     def pack(put, up_ref, dn_ref):
         each(L // 4, 2, lambda g: pack_rows([put(4 * g + k) for k in range(4)], g, up_ref, dn_ref))
 
+    def beside_rows(a_ref, b_ref, g):
+        a = a_ref[g]
+        b = b_ref[g]
+        out = []
+        for k in range(4):
+            ra = pltpu.roll(a, 6 - 2 * k, 0) if k < 3 else a
+            rb = pltpu.roll(b, 8 - 2 * k, 0) if k else b
+            out.append(jnp.where(sub >= 4, ra, rb))
+        return out
+
     def unpack(a_ref, b_ref, write):
         def body(g):
-            a = a_ref[g]
-            b = b_ref[g]
-            for k in range(4):
-                ra = pltpu.roll(a, 6 - 2 * k, 0) if k < 3 else a
-                rb = pltpu.roll(b, 8 - 2 * k, 0) if k else b
-                write(4 * g + k, jnp.where(sub >= 4, ra, rb))
+            for k, x in enumerate(beside_rows(a_ref, b_ref, g)):
+                write(4 * g + k, x)
         each(L // 4, 2, body)
+
+    def pack_outer(rows, g, up_ref, dn_ref):
+        up = rows[7]
+        dn = pltpu.roll(rows[7], 7, 0)
+        for k in range(6, -1, -1):
+            up = jnp.where(sub <= k, pltpu.roll(rows[k], k + 1, 0), up)
+            dn = jnp.where(sub <= k, pltpu.roll(rows[k], k, 0) if k else rows[k], dn)
+        up_ref[g] = up
+        dn_ref[g] = dn
+
+    def beside_outer(a_ref, b_ref, g):
+        a = a_ref[g]
+        b = b_ref[g]
+        out = []
+        for k in range(8):
+            ra = pltpu.roll(a, 7 - k, 0) if k < 7 else a
+            rb = pltpu.roll(b, 8 - k, 0) if k else b
+            out.append(jnp.where(sub >= 4, ra, rb))
+        return out
 
     first_lane = lane_h == 0
     last_lane = lane_h == 127
@@ -178,12 +203,14 @@
             return g
         return last, loop(L, 8, again, zero)
 
-    def solve(read, m_ref, f_ref, y_ref):
-        def fwd(l, f):
-            f = 0.5 * read(l) + m_ref[l] * f
-            f_ref[l] = f
+    def solve(read, size, m_ref, f_ref, y_ref):
+        def fwd(g, f):
+            for k, r in enumerate(read(g)):
+                l = g * size + k
+                f = 0.5 * r + m_ref[l] * f
+                f_ref[l] = f
             return f
-        first = loop(L, 16, fwd, zero)
+        first = loop(L // size, 16 // size, fwd, zero)
 
         def back(k, y):
             l = L - 1 - k
@@ -193,8 +220,8 @@
         loop(L, 16, back, zero)
         return first
 
-    def passes(read, m_ref, f_ref):
-        first = solve(read, m_ref, f_ref, y_f)
+    def passes(read, size, m_ref, f_ref):
+        first = solve(read, size, m_ref, f_ref, y_f)
 
         def again(l, g):
             g = 0.5 * y_f[l] + m_ref[l] * g
@@ -253,6 +280,19 @@
         if j < STEPS - 1:
             body(L)
 
+    def outer_dots(j):
+        def body(l, carry):
+            b = v_h[l + 1]
+            add = jnp.where(sub == 0, pltpu.roll(b, 1, 0), jnp.where(sub == 7, pltpu.roll(b, 7, 0), 0.0))
+            u = u_m[j, l + 1] - add
+            u_m[j, l + 1] = u
+            out = [carry[i] + u * u_m[i, l + 1] for i in range(j)]
+            return tuple(out + [carry[j] + u * u])
+        sums = loop(L, 8, body, (zero,) * (j + 1))
+        for i in range(j + 1):
+            n = ROW[i, j]
+            gram[n:n + 1] = fold(sums[i])
+
     def outer_k(j):
         def fix(l, b):
             add = jnp.where(sub == 0, pltpu.roll(b, 1, 0), jnp.where(sub == 7, pltpu.roll(b, 7, 0), 0.0))
@@ -261,12 +301,10 @@
         def body(l):
             b = v_h[l + 1]
             fix(l, b)
-            if j < STEPS - 1:
-                u = (d_h[l] * b - beside(b, v_m[j, l + 1])) - 2.0 * (v_h[l] + v_h[l + 2])
-                u_h[l] = mask_h * u
+            u = (d_h[l] * b - beside(b, v_m[j, l + 1])) - 2.0 * (v_h[l] + v_h[l + 2])
+            u_h[l] = mask_h * u
         each(L, 8, body)
-        if j < STEPS - 1:
-            fix(L, v_h[L + 1])
+        fix(L, v_h[L + 1])
 
     def again_k(j, l):
         a = u_m[j, l + 1]
@@ -281,18 +319,18 @@
             total = total + row[:, n * 128:(n + 1) * 128]
         return total
 
+    def side_dot(j):
+        n = len(PAIRS) + j
+        gram[n:n + 1] = fold(loop(L, 8, lambda l, acc: acc + v_m[j, l + 1] * s_m[l + 1], zero))
+
     def dots(j):
         def body(l, carry):
             u = u_m[j, l + 1]
-            out = [carry[0] + v_m[j, l + 1] * s_m[l + 1]]
-            for i in range(j + 1):
-                out.append(carry[i + 1] + u * u_m[i, l + 1])
-            return tuple(out)
-        sums = loop(L, 8, body, (zero,) * (j + 2))
-        gram[len(PAIRS) + j:len(PAIRS) + j + 1] = fold(sums[0])
+            return tuple(carry[i] + u * u_m[i, l + 1] for i in range(j + 1))
+        sums = loop(L, 8, body, (zero,) * (j + 1))
         for i in range(j + 1):
             n = ROW[i, j]
-            gram[n:n + 1] = fold(sums[i + 1])
+            gram[n:n + 1] = fold(sums[i])
 
     low = lane_h < 64
 
@@ -327,9 +365,13 @@
         return d
     pack(put_d, halo_out.at[0, 0], halo_out.at[0, 1])
     pl.semaphore_wait(barrier, len(greet))
+    G2 = L // 8
+    in_pair = lax.rem(probe, 2)
+    part = pl.ds(in_pair * G2, G2)
+    pair = {"probe": probe + 1 - 2 * in_pair}
     halo_d = [
-        post(halo_out.at[0, 0], halo_in.at[0, 0], {"tile": nxt}),
-        post(halo_out.at[0, 1], halo_in.at[0, 1], {"tile": prv}),
+        post(halo_out.at[0, 0, part], halo_in.at[0, 0, part], {"tile": nxt}),
+        post(halo_out.at[0, 1, part], halo_in.at[0, 1, part], {"tile": prv}),
     ]
     mo_m, ho_m = factor(d_m, m_m, hg_m)
     loads[1].wait()
@@ -339,7 +381,7 @@
         s_m[l + 1] = s
         return s
     pack(put_s, halo_out.at[1, 0], halo_out.at[1, 1])
-    own_m = passes(lambda l: s_m[l + 1], m_m, f_m)
+    own_m = passes(lambda l: [s_m[l + 1]], 1, m_m, f_m)
     loads[2].wait()
     side_out[0] = edges(mo_m, ho_m)
     side_out[1] = edges(own_m[0], own_m[1])
@@ -376,9 +418,13 @@
         al_m[l] = x
         return m_m[l] * x
     loop(L, 16, weigh, zero + 0.5)
-    solve(lambda l: al_m[l], m_m, r_m, be_m)
-
-    for copy in halo_d:
+    solve(lambda l: [al_m[l]], 1, m_m, r_m, be_m)
+
+    shared = []
+    for side, copy in enumerate(halo_d):
+        copy.wait_recv()
+        shared.append(post(halo_in.at[0, side, part], halo_in.at[0, side, part], pair))
+    for copy in shared:
         copy.wait_recv()
 
     def put_dh(l, x):
@@ -398,10 +444,12 @@
     for copy in halo_s:
         copy.wait_recv()
 
-    def put_sh(l, x):
-        s_h[l] = x * mask_h
-    unpack(halo_in.at[1, 0], halo_in.at[1, 1], put_sh)
-    own_h = passes(lambda l: s_h[l], m_h, f_h)
+    def read_sh(g):
+        rows = [x * mask_h for x in beside_rows(halo_in.at[1, 0], halo_in.at[1, 1], g)]
+        for k, x in enumerate(rows):
+            s_h[4 * g + k] = x
+        return rows
+    own_h = passes(read_sh, 4, m_h, f_h)
     for copy in far[:2]:
         copy.wait_recv()
 
@@ -442,19 +490,22 @@
 
     for j in range(1, STEPS):
         n = j - 1
+        one_row = j == STEPS - 1 and L % 8 == 0
+        size = 8 if one_row else 4
+        used = pl.ds(0, L // size)
 
         def form(g, carry):
             fo, go = carry
             tiles_r = []
-            for k in range(4):
-                l = 4 * g + k
+            for k in range(size):
+                l = size * g + k
                 r = again_k(j - 1, l)
                 fo = fo + al_m[l] * r
                 go = go + be_m[l] * r
                 tiles_r.append(r)
-            pack_rows(tiles_r, g, xs_out.at[n, 0], xs_out.at[n, 1])
+            (pack_outer if one_row else pack_rows)(tiles_r, g, xs_out.at[n, 0], xs_out.at[n, 1])
             return fo, go
-        own_m = loop(L // 4, 2, form, (zero, zero))
+        own_m = loop(L // size, 8 // size, form, (zero, zero))
         ed_out[n] = edges(own_m[0], own_m[1])
         pl_out[n, 0] = own_m[0]
         pl_out[n, 1] = own_m[1]
@@ -464,13 +515,14 @@
             post(pl_out.at[n], pl_in.at[n], {"level": other}),
         ]
         rows = [
-            post(xs_out.at[n, 0], xs_in.at[n, 0], {"tile": nxt}),
-            post(xs_out.at[n, 1], xs_in.at[n, 1], {"tile": prv}),
+            post(xs_out.at[n, 0, used], xs_in.at[n, 0, used], {"tile": nxt}),
+            post(xs_out.at[n, 1, used], xs_in.at[n, 1, used], {"tile": prv}),
         ]
         for dev in z_beside:
             pl.semaphore_signal(here_sem.at[n], inc=1, device_id=dev, device_id_type=MESH)
-        passes(lambda l: r_m[l], m_m, f_m)
+        passes(lambda l: [r_m[l]], 1, m_m, f_m)
         dots(j - 1)
+        side_dot(j - 1)
         if j == 1:
             side_terms()
         if j == 2:
@@ -479,13 +531,18 @@
         planes[2].wait_recv()
         finish_m(j, const_m, own_m, (pl_in[n, 0], pl_in[n, 1]), dp_m)
         inner_k(j)
+        if j == STEPS - 1:
+            side_dot(j)
+            for i in range(len(PAIRS) + STEPS, N_ROWS):
+                gram[i:i + 1] = jnp.zeros((1, 128), F32)
         for copy in rows:
             copy.wait_recv()
 
-        def put_rh(l, x):
-            r_h[l] = x * mask_h
-        unpack(xs_in.at[n, 0], xs_in.at[n, 1], put_rh)
-        own_h = passes(lambda l: r_h[l], m_h, f_h)
+        beside_r = beside_outer if one_row else beside_rows
+
+        def read_rh(g):
+            return [x * mask_h for x in beside_r(xs_in.at[n, 0], xs_in.at[n, 1], g)]
+        own_h = passes(read_rh, size, m_h, f_h)
         for copy in planes[:2]:
             copy.wait_recv()
         if z_beside:
@@ -493,10 +550,10 @@
         send_t(j - 1)
         fp_h, gp_h = beyond(ed_in[n, 0], ed_in[n, 1])
         finish_h(j, const_h, own_h, (mask_h * fp_h, mask_h * gp_h))
-        outer_k(j)
-    for n in range(len(PAIRS) + STEPS, N_ROWS):
-        gram[n:n + 1] = jnp.zeros((1, 128), F32)
-    dots(STEPS - 1)
+        if j < STEPS - 1:
+            outer_k(j)
+        else:
+            outer_dots(j)
 
     wide = lax.broadcasted_iota(jnp.int32, (N_ROWS, 128), 1) == lax.broadcasted_iota(jnp.int32, (N_ROWS, 128), 0)
     each_sum = jnp.sum(gram[...], axis=1, keepdims=True)
@@ -578,13 +635,13 @@
         vm = lambda *lead: pltpu.VMEM((*lead, 8, Y), F32)
         dma = lambda n: pltpu.SemaphoreType.DMA((n,))
         G = L // 4
-        n_sems = 9 + 5 * (STEPS - 1) + (probes * levels * x_chips - 1) + (z_chips - 1) + STEPS * (probes - 1)
+        n_sems = 11 + 5 * (STEPS - 1) + (probes * levels * x_chips - 1) + (z_chips - 1) + STEPS * (probes - 1)
         part = lambda *lead: pltpu.VMEM((*lead, L // 2, 8, 128), F32)
         scratch = [
             pltpu.VMEM((L, 8, Y), jnp.int32), vm(L), vm(L),
             vm(L + 2), vm(L), vm(L + 1), vm(L), vm(L + 2), vm(L),
             vm(L + 1), vm(L + 1), vm(L), vm(L), vm(L), vm(L),
-            vm(STEPS, L + 3), vm(L + 2), vm(STEPS, L + 2), vm(L), vm(L), vm(L), vm(L), vm(L), vm(L), vm(L),
+            vm(STEPS, L + 3), vm(L + 2), vm(STEPS, L + 2), vm(L), vm(L), vm(L), vm(L), vm(L), vm(L),
             vm(3, 2, G), vm(3, 2, G), vm(STEPS - 1, 2, G), vm(STEPS - 1, 2, G),
             vm(7), vm(7), vm(2), vm(2, 2),
             vm(STEPS - 1, 2), vm(STEPS - 1, 2), vm(STEPS - 1), vm(STEPS - 1, 2),

time: 49 us -> 49.1 us (level)
  no operation moved by 1% of the time
where the time goes in v5:
time: 49.1 us; the launch traced here: 49 us
  Pallas kernels  48.3 us (98%)
  local copies, waits for them, and re-layouts  0.66 us (1%)
    pallas_call x1, Pallas kernels, step(): pl.pallas_call(functools.partial(kernel, dims), out_shape=pltpu.VMEM((L,...  48.3 us

profile of v5, /device:TPU:1, one launch (start us, length us, event | category | flops | bytes accessed | tf_op | source)
XLA Modules:
  0.0 49.0 jit_solution(16042970523503450021)
XLA Ops:
  0.0 48.3 %shard_map.37 = f32[32,8,64]{2,1,0:T(8,128)S(1)} custom-call(s32[1,32,8,256]{3,2,1,0:T(8,128)} %bits_hbm.1, f32[32,8,256]{2,1,0:T(8,128)} %kap_hbm.1, f32[32,8,256]{2,1,0:T(8,128)} %obs_hbm.1), custom_call_target="tpu_custom_call" | custom-call | tf_op jit(solution)/shard_map/pallas_call | solution.py:655
  48.3 0.7 %copy.5 = f32[32,8,64]{2,1,0:T(8,128)} copy(f32[32,8,64]{2,1,0:T(8,128)S(1)} %shard_map.37) | data formatting | bytes 131072

commit v6 on v5

--- a/solution.py
+++ b/solution.py
@@ -60,14 +60,26 @@
                for t in near_x + [tile] for h in (other, half) for p in near_p + [probe]][:-1]
     b_peers = [{"tile": lax.rem(tile + k * x_chips, tiles)} for k in around(z_chips)]
     p_peers = near_p
-    z_beside = [{"tile": lax.rem(tile + x_chips, tiles)}, {"tile": lax.rem(tile + tiles - x_chips, tiles)}]
-    if z_chips == 1:
-        z_beside = []
+    not_end = [tile < tiles - 1, tile > 0]
+
+    def along_z(d):
+        return [(zc + d < z_chips, {"tile": lax.rem(tile + d * x_chips, tiles)}),
+                (zc >= d, {"tile": lax.rem(tile + tiles - d * x_chips, tiles)})]
+
+    def signal_if(sem, pairs):
+        for there, dev in pairs:
+            pl.when(there)(functools.partial(
+                pl.semaphore_signal, sem, inc=1, device_id=dev, device_id_type=MESH))
+
+    def count(pairs):
+        return sum(there.astype(jnp.int32) for there, _ in pairs)
 
     barrier = pltpu.get_barrier_semaphore()
-    greet = [{"tile": nxt}, {"tile": prv}, {"level": other},
-             {"tile": nxt, "level": other}, {"tile": prv, "level": other}]
-    greet += [{"probe": p} for p in p_peers] + z_beside
+    ends = [(not_end[0], {"tile": nxt}), (not_end[1], {"tile": prv}),
+            (not_end[0], {"tile": nxt, "level": other}), (not_end[1], {"tile": prv, "level": other})]
+    ends += along_z(1)
+    greet = [{"level": other}] + [{"probe": p} for p in p_peers]
+    signal_if(barrier, ends)
     for dev in greet:
         pl.semaphore_signal(barrier, inc=1, device_id=dev, device_id_type=MESH)
 
@@ -96,6 +108,27 @@
         n = counter[0]
         counter[0] += 1
         copy = send(src_ref, dst_ref, send_sem.at[n], recv_sem.at[n], dev)
+        started.append(copy)
+        return copy
+
+    class Ended:
+        def __init__(self, copy, goes, comes):
+            self.copy, self.goes, self.comes = copy, goes, comes
+            pl.when(goes)(copy.start)
+
+        def wait_send(self):
+            pl.when(self.goes)(self.copy.wait_send)
+
+        def wait_recv(self):
+            pl.when(self.comes)(self.copy.wait_recv)
+
+    def post_to(side, src_ref, dst_ref, dev):
+        n = counter[0]
+        counter[0] += 1
+        copy = pltpu.make_async_remote_copy(
+            src_ref=src_ref, dst_ref=dst_ref, send_sem=send_sem.at[n], recv_sem=recv_sem.at[n],
+            device_id=dev, device_id_type=MESH)
+        copy = Ended(copy, not_end[side], not_end[1 - side])
         started.append(copy)
         return copy
 
@@ -359,19 +392,29 @@
 
     loads[0].wait()
 
+    for side in range(2):
+        @pl.when(jnp.logical_not(not_end[1 - side]))
+        def _():
+            def clear(g):
+                for k in range(3):
+                    halo_in[k, side, g] = zero
+                for k in range(STEPS - 1):
+                    xs_in[k, side, g] = zero
+            each(L // 4, 1, clear)
+            for k in range(2):
+                side_in[side, k] = zero
+            for k in range(STEPS - 1):
+                ed_in[k, side] = zero
+
     def put_d(l):
         d = kap_v[src(l)] + 8.0
         d_m[l] = d
         return d
     pack(put_d, halo_out.at[0, 0], halo_out.at[0, 1])
-    pl.semaphore_wait(barrier, len(greet))
-    G2 = L // 8
-    in_pair = lax.rem(probe, 2)
-    part = pl.ds(in_pair * G2, G2)
-    pair = {"probe": probe + 1 - 2 * in_pair}
+    pl.semaphore_wait(barrier, len(greet) + count(ends))
     halo_d = [
-        post(halo_out.at[0, 0, part], halo_in.at[0, 0, part], {"tile": nxt}),
-        post(halo_out.at[0, 1, part], halo_in.at[0, 1, part], {"tile": prv}),
+        post_to(0, halo_out.at[0, 0], halo_in.at[0, 0], {"tile": nxt}),
+        post_to(1, halo_out.at[0, 1], halo_in.at[0, 1], {"tile": prv}),
     ]
     mo_m, ho_m = factor(d_m, m_m, hg_m)
     loads[1].wait()
@@ -388,13 +431,13 @@
     for n, plane in enumerate((mo_m, ho_m, own_m[0], own_m[1], d_m[L - 1], s_m[L], obs_v[src(L - 1)])):
         first_out[n] = plane
     far = [
-        post(side_out, side_in.at[0], {"tile": nxt, "level": other}),
-        post(side_out, side_in.at[1], {"tile": prv, "level": other}),
+        post_to(0, side_out, side_in.at[0], {"tile": nxt, "level": other}),
+        post_to(1, side_out, side_in.at[1], {"tile": prv, "level": other}),
         post(first_out, first_in, {"level": other}),
     ]
     halo_s = [
-        post(halo_out.at[1, 0], halo_in.at[1, 0], {"tile": nxt}),
-        post(halo_out.at[1, 1], halo_in.at[1, 1], {"tile": prv}),
+        post_to(0, halo_out.at[1, 0], halo_in.at[1, 0], {"tile": nxt}),
+        post_to(1, halo_out.at[1, 1], halo_in.at[1, 1], {"tile": prv}),
     ]
     s_m[0] = zero
     o_m[0] = zero
@@ -409,8 +452,8 @@
         return o
     pack(put_o, halo_out.at[2, 0], halo_out.at[2, 1])
     halo_o = [
-        post(halo_out.at[2, 0], halo_in.at[2, 0], {"tile": nxt}),
-        post(halo_out.at[2, 1], halo_in.at[2, 1], {"tile": prv}),
+        post_to(0, halo_out.at[2, 0], halo_in.at[2, 0], {"tile": nxt}),
+        post_to(1, halo_out.at[2, 1], halo_in.at[2, 1], {"tile": prv}),
     ]
 
     def weigh(k, x):
@@ -420,11 +463,7 @@
     loop(L, 16, weigh, zero + 0.5)
     solve(lambda l: [al_m[l]], 1, m_m, r_m, be_m)
 
-    shared = []
-    for side, copy in enumerate(halo_d):
-        copy.wait_recv()
-        shared.append(post(halo_in.at[0, side, part], halo_in.at[0, side, part], pair))
-    for copy in shared:
+    for copy in halo_d:
         copy.wait_recv()
 
     def put_dh(l, x):
@@ -510,16 +549,15 @@
         pl_out[n, 0] = own_m[0]
         pl_out[n, 1] = own_m[1]
         planes = [
-            post(ed_out.at[n], ed_in.at[n, 0], {"tile": nxt, "level": other}),
-            post(ed_out.at[n], ed_in.at[n, 1], {"tile": prv, "level": other}),
+            post_to(0, ed_out.at[n], ed_in.at[n, 0], {"tile": nxt, "level": other}),
+            post_to(1, ed_out.at[n], ed_in.at[n, 1], {"tile": prv, "level": other}),
             post(pl_out.at[n], pl_in.at[n], {"level": other}),
         ]
         rows = [
-            post(xs_out.at[n, 0, used], xs_in.at[n, 0, used], {"tile": nxt}),
-            post(xs_out.at[n, 1, used], xs_in.at[n, 1, used], {"tile": prv}),
+            post_to(0, xs_out.at[n, 0, used], xs_in.at[n, 0, used], {"tile": nxt}),
+            post_to(1, xs_out.at[n, 1, used], xs_in.at[n, 1, used], {"tile": prv}),
         ]
-        for dev in z_beside:
-            pl.semaphore_signal(here_sem.at[n], inc=1, device_id=dev, device_id_type=MESH)
+        signal_if(here_sem.at[n], along_z(2 ** n))
         passes(lambda l: [r_m[l]], 1, m_m, f_m)
         dots(j - 1)
         side_dot(j - 1)
@@ -545,8 +583,7 @@
         own_h = passes(read_rh, size, m_h, f_h)
         for copy in planes[:2]:
             copy.wait_recv()
-        if z_beside:
-            pl.semaphore_wait(here_sem.at[n], len(z_beside))
+        pl.semaphore_wait(here_sem.at[n], count(along_z(2 ** n)))
         send_t(j - 1)
         fp_h, gp_h = beyond(ed_in[n, 0], ed_in[n, 1])
         finish_h(j, const_h, own_h, (mask_h * fp_h, mask_h * gp_h))
@@ -635,7 +672,7 @@
         vm = lambda *lead: pltpu.VMEM((*lead, 8, Y), F32)
         dma = lambda n: pltpu.SemaphoreType.DMA((n,))
         G = L // 4
-        n_sems = 11 + 5 * (STEPS - 1) + (probes * levels * x_chips - 1) + (z_chips - 1) + STEPS * (probes - 1)
+        n_sems = 9 + 5 * (STEPS - 1) + (probes * levels * x_chips - 1) + (z_chips - 1) + STEPS * (probes - 1)
         part = lambda *lead: pltpu.VMEM((*lead, L // 2, 8, 128), F32)
         scratch = [
             pltpu.VMEM((L, 8, Y), jnp.int32), vm(L), vm(L),

time: 49.1 us -> 48.8 us (level)
  no operation moved by 1% of the time
where the time goes in v6:
time: 48.8 us; the launch traced here: 48.7 us
  Pallas kernels  48.1 us (99%)
  local copies, waits for them, and re-layouts  0.66 us (1%)
    pallas_call x1, Pallas kernels, step(): pl.pallas_call(functools.partial(kernel, dims), out_shape=pltpu.VMEM((L,...  48.1 us

profile of v6, /device:TPU:1, one launch (start us, length us, event | category | flops | bytes accessed | tf_op | source)
XLA Modules:
  0.0 48.7 jit_solution(4293368349897341999)
XLA Ops:
  0.0 48.1 %shard_map.37 = f32[32,8,64]{2,1,0:T(8,128)S(1)} custom-call(s32[1,32,8,256]{3,2,1,0:T(8,128)} %bits_hbm.1, f32[32,8,256]{2,1,0:T(8,128)} %kap_hbm.1, f32[32,8,256]{2,1,0:T(8,128)} %obs_hbm.1), custom_call_target="tpu_custom_call" | custom-call | tf_op jit(solution)/shard_map/pallas_call | solution.py:692
  48.1 0.7 %copy.5 = f32[32,8,64]{2,1,0:T(8,128)} copy(f32[32,8,64]{2,1,0:T(8,128)S(1)} %shard_map.37) | data formatting | bytes 131072

commit v7 on v6

--- a/solution.py
+++ b/solution.py
@@ -23,7 +23,7 @@
     bits_v, kap_v, obs_v,
     s_m, s_h, d_m, d_h, o_m, o_h,
     m_m, m_h, hg_m, hg_h, al_m, be_m,
-    v_m, v_h, u_m, u_h, r_m, f_m, f_h, y_f, ks,
+    v_m, v_h, u_m, r_m, f_m, f_h, y_f, ks,
     halo_out, halo_in, xs_out, xs_in,
     first_out, first_in, side_out, side_in, pl_out, pl_in, ed_out, ed_in,
     gram, red_out, red_a, red_b, t_out, t_in, kap_q, sub_q, data,
@@ -236,14 +236,20 @@
             return g
         return last, loop(L, 8, again, zero)
 
-    def solve(read, size, m_ref, f_ref, y_ref):
+    def solve(read, size, m_ref, f_ref, y_ref, waits=()):
         def fwd(g, f):
             for k, r in enumerate(read(g)):
                 l = g * size + k
                 f = 0.5 * r + m_ref[l] * f
                 f_ref[l] = f
             return f
-        first = loop(L // size, 16 // size, fwd, zero)
+        pieces = max(len(waits), 1)
+        per = L // size // pieces
+        first = zero
+        for p in range(pieces):
+            for copy in waits[p] if waits else ():
+                copy.wait_recv()
+            first = loop(per, max(16 // size, 1), functools.partial(lambda at, g, f: fwd(at + g, f), p * per), first)
 
         def back(k, y):
             l = L - 1 - k
@@ -253,8 +259,8 @@
         loop(L, 16, back, zero)
         return first
 
-    def passes(read, size, m_ref, f_ref):
-        first = solve(read, size, m_ref, f_ref, y_f)
+    def passes(read, size, m_ref, f_ref, waits=()):
+        first = solve(read, size, m_ref, f_ref, y_f, waits)
 
         def again(l, g):
             g = 0.5 * y_f[l] + m_ref[l] * g
@@ -326,24 +332,60 @@
             n = ROW[i, j]
             gram[n:n + 1] = fold(sums[i])
 
-    def outer_k(j):
-        def fix(l, b):
-            add = jnp.where(sub == 0, pltpu.roll(b, 1, 0), jnp.where(sub == 7, pltpu.roll(b, 7, 0), 0.0))
-            u_m[j, l + 1] = u_m[j, l + 1] - add
-
-        def body(l):
+    def one_row(j):
+        return j == STEPS - 2 and L % 16 == 0
+
+    def advance(j):
+        size = 8 if one_row(j) else 4
+        per = L // size // 2
+        wrap = pack_outer if one_row(j) else pack_rows
+
+        def settle(l):
             b = v_h[l + 1]
-            fix(l, b)
-            u = (d_h[l] * b - beside(b, v_m[j, l + 1])) - 2.0 * (v_h[l] + v_h[l + 2])
-            u_h[l] = mask_h * u
-        each(L, 8, body)
-        fix(L, v_h[L + 1])
-
-    def again_k(j, l):
-        a = u_m[j, l + 1]
-        r = (d_m[l] * a - beside(a, u_h[l])) - 2.0 * (u_m[j, l] + u_m[j, l + 2])
-        r_m[l] = r
-        return r
+            a = v_m[j, l + 1]
+            from_up, from_dn = pltpu.roll(b, 1, 0), pltpu.roll(b, 7, 0)
+            u = u_m[j, l + 1] - jnp.where(sub == 0, from_up, jnp.where(sub == 7, from_dn, 0.0))
+            u_m[j, l + 1] = u
+            up = jnp.where(sub == 0, pltpu.roll(a, 1, 0), from_up)
+            dn = jnp.where(sub == 7, pltpu.roll(a, 7, 0), from_dn)
+            outer = (d_h[l] * b - ((up + dn) + sides(b))) - 2.0 * (v_h[l] + v_h[l + 2])
+            return u, mask_h * outer
+
+        def form(g, carry):
+            before, here, outer, fo, go = carry
+            tiles_r = []
+            for k in range(size):
+                l = size * g + k
+                after, next_outer = settle(l + 1)
+                r = (d_m[l] * here - beside(here, outer)) - 2.0 * (before + after)
+                r_m[l] = r
+                fo = fo + al_m[l] * r
+                go = go + be_m[l] * r
+                tiles_r.append(r)
+                before, here, outer = here, after, next_outer
+            wrap(tiles_r, g, xs_out.at[j, 0], xs_out.at[j, 1])
+            return before, here, outer, fo, go
+
+        state = (zero,) + settle(0) + (zero, zero)
+        rows = []
+        for p in range(2):
+            state = loop(per, 8 // size, functools.partial(lambda at, g, c: form(at + g, c), p * per), state)
+            if p == 1:
+                own = state[3:]
+                ed_out[j] = edges(own[0], own[1])
+                pl_out[j, 0] = own[0]
+                pl_out[j, 1] = own[1]
+                planes = [
+                    post_to(0, ed_out.at[j], ed_in.at[j, 0], {"tile": nxt, "level": other}),
+                    post_to(1, ed_out.at[j], ed_in.at[j, 1], {"tile": prv, "level": other}),
+                    post(pl_out.at[j], pl_in.at[j], {"level": other}),
+                ]
+            cut = pl.ds(p * per, per)
+            rows.append([
+                post_to(0, xs_out.at[j, 0, cut], xs_in.at[j, 0, cut], {"tile": nxt}),
+                post_to(1, xs_out.at[j, 1, cut], xs_in.at[j, 1, cut], {"tile": prv}),
+            ])
+        return own, planes, rows
 
     def fold(acc):
         row = jnp.sum(acc, axis=0, keepdims=True)
@@ -445,6 +487,8 @@
         v_m[j, 0] = zero
         u_m[j, 0] = zero
     v_h[0] = zero
+    v_h[L + 2] = zero
+    d_h[L] = zero
 
     def put_o(l):
         o = obs_v[src(l)]
@@ -496,7 +540,7 @@
     fp_h, gp_h = beyond(side_in[0, 1], side_in[1, 1])
     const_h = (mo_h, ho_h, mp_h, hp_h, 1.0 / (1.0 - mo_h * mp_h))
     finish_h(0, const_h, own_h, (mask_h * fp_h, mask_h * gp_h))
-    outer_k(0)
+    own_m, planes, rows = advance(0)
 
     odd = lax.rem(probe, 2) == 1
     upper = probe // 2 == 1
@@ -529,34 +573,6 @@
 
     for j in range(1, STEPS):
         n = j - 1
-        one_row = j == STEPS - 1 and L % 8 == 0
-        size = 8 if one_row else 4
-        used = pl.ds(0, L // size)
-
-        def form(g, carry):
-            fo, go = carry
-            tiles_r = []
-            for k in range(size):
-                l = size * g + k
-                r = again_k(j - 1, l)
-                fo = fo + al_m[l] * r
-                go = go + be_m[l] * r
-                tiles_r.append(r)
-            (pack_outer if one_row else pack_rows)(tiles_r, g, xs_out.at[n, 0], xs_out.at[n, 1])
-            return fo, go
-        own_m = loop(L // size, 8 // size, form, (zero, zero))
-        ed_out[n] = edges(own_m[0], own_m[1])
-        pl_out[n, 0] = own_m[0]
-        pl_out[n, 1] = own_m[1]
-        planes = [
-            post_to(0, ed_out.at[n], ed_in.at[n, 0], {"tile": nxt, "level": other}),
-            post_to(1, ed_out.at[n], ed_in.at[n, 1], {"tile": prv, "level": other}),
-            post(pl_out.at[n], pl_in.at[n], {"level": other}),
-        ]
-        rows = [
-            post_to(0, xs_out.at[n, 0, used], xs_in.at[n, 0, used], {"tile": nxt}),
-            post_to(1, xs_out.at[n, 1, used], xs_in.at[n, 1, used], {"tile": prv}),
-        ]
         signal_if(here_sem.at[n], along_z(2 ** n))
         passes(lambda l: [r_m[l]], 1, m_m, f_m)
         dots(j - 1)
@@ -573,14 +589,11 @@
             side_dot(j)
             for i in range(len(PAIRS) + STEPS, N_ROWS):
                 gram[i:i + 1] = jnp.zeros((1, 128), F32)
-        for copy in rows:
-            copy.wait_recv()
-
-        beside_r = beside_outer if one_row else beside_rows
+        beside_r = beside_outer if one_row(j - 1) else beside_rows
 
         def read_rh(g):
             return [x * mask_h for x in beside_r(xs_in.at[n, 0], xs_in.at[n, 1], g)]
-        own_h = passes(read_rh, size, m_h, f_h)
+        own_h = passes(read_rh, 8 if one_row(j - 1) else 4, m_h, f_h, rows)
         for copy in planes[:2]:
             copy.wait_recv()
         pl.semaphore_wait(here_sem.at[n], count(along_z(2 ** n)))
@@ -588,7 +601,7 @@
         fp_h, gp_h = beyond(ed_in[n, 0], ed_in[n, 1])
         finish_h(j, const_h, own_h, (mask_h * fp_h, mask_h * gp_h))
         if j < STEPS - 1:
-            outer_k(j)
+            own_m, planes, rows = advance(j)
         else:
             outer_dots(j)
 
@@ -672,13 +685,13 @@
         vm = lambda *lead: pltpu.VMEM((*lead, 8, Y), F32)
         dma = lambda n: pltpu.SemaphoreType.DMA((n,))
         G = L // 4
-        n_sems = 9 + 5 * (STEPS - 1) + (probes * levels * x_chips - 1) + (z_chips - 1) + STEPS * (probes - 1)
+        n_sems = 9 + 7 * (STEPS - 1) + (probes * levels * x_chips - 1) + (z_chips - 1) + STEPS * (probes - 1)
         part = lambda *lead: pltpu.VMEM((*lead, L // 2, 8, 128), F32)
         scratch = [
             pltpu.VMEM((L, 8, Y), jnp.int32), vm(L), vm(L),
-            vm(L + 2), vm(L), vm(L + 1), vm(L), vm(L + 2), vm(L),
+            vm(L + 2), vm(L), vm(L + 1), vm(L + 1), vm(L + 2), vm(L),
             vm(L + 1), vm(L + 1), vm(L), vm(L), vm(L), vm(L),
-            vm(STEPS, L + 3), vm(L + 2), vm(STEPS, L + 2), vm(L), vm(L), vm(L), vm(L), vm(L), vm(L),
+            vm(STEPS, L + 3), vm(L + 3), vm(STEPS, L + 2), vm(L), vm(L), vm(L), vm(L), vm(L),
             vm(3, 2, G), vm(3, 2, G), vm(STEPS - 1, 2, G), vm(STEPS - 1, 2, G),
             vm(7), vm(7), vm(2), vm(2, 2),
             vm(STEPS - 1, 2), vm(STEPS - 1, 2), vm(STEPS - 1), vm(STEPS - 1, 2),

time: 48.8 us -> 48.8 us (level)
  no operation moved by 1% of the time
where the time goes in v7:
time: 48.8 us; the launch traced here: 48.7 us
  Pallas kernels  48 us (98%)
  local copies, waits for them, and re-layouts  0.66 us (1%)
    pallas_call x1, Pallas kernels, step(): pl.pallas_call(functools.partial(kernel, dims), out_shape=pltpu.VMEM((L,...  48 us

profile of v7, /device:TPU:1, one launch (start us, length us, event | category | flops | bytes accessed | tf_op | source)
XLA Modules:
  0.0 48.7 jit_solution(10953782750867009138)
XLA Ops:
  0.0 48.0 %shard_map.37 = f32[32,8,64]{2,1,0:T(8,128)S(1)} custom-call(s32[1,32,8,256]{3,2,1,0:T(8,128)} %bits_hbm.1, f32[32,8,256]{2,1,0:T(8,128)} %kap_hbm.1, f32[32,8,256]{2,1,0:T(8,128)} %obs_hbm.1), custom_call_target="tpu_custom_call" | custom-call | tf_op jit(solution)/shard_map/pallas_call | solution.py:705
  48.0 0.7 %copy.5 = f32[32,8,64]{2,1,0:T(8,128)} copy(f32[32,8,64]{2,1,0:T(8,128)S(1)} %shard_map.37) | data formatting | bytes 131072
